TPU v7x, 512 devices: a whole 4x8x8 slice. The times are simulated.
512 devices in a mesh: req: 128 (over z, y, core), tp: 4 (over x).
Axes of the slice: x: 4, y: 8, z: 8, core: 2. Of those that a mesh axis runs over, the one named last changes fastest.
Arguments:
- tokens: bfloat16 [49152, 3200], P('req'), may hold values from -6 to 6
- norm_gain: float32 [3200], replicated, may hold values from 0.5 to 2
- w_qkv: bfloat16 [3200, 6144], P('req', 'tp'), may hold values from -1 to 1
- q_gain: float32 [2048], P('tp'), may hold values from 0.5 to 2.5
- k_gain: float32 [2048], P('tp'), may hold values from 0.5 to 2.5
- w_out: bfloat16 [2048, 3200], P('tp', 'req'), may hold values from -0.125 to 0.125
- grids: int32 [384, 2], P('req'), may hold values from 2 to 16, as said below
- owners: int32 [12288], P('req'), may hold values from 0 to 127, as said below
- proj_gain: float32 [4, 3200], P(None, 'tp'), may hold values from 0.5 to 2
- proj_bias: float32 [4, 3200], P(None, 'tp'), may hold values from -3 to 3
Outputs:
- received: bfloat16 [32768, 4, 3200], P('req', None, 'tp')
Inputs may be any that keep to these rules, and one draw needn't show every extreme that they name: `grids`: each image spans at least 2 half grid rows. The images of one device together take at most 96 merged slots, and on one device in every draw exactly 96. `owners`: no device's merged slots, live or padding, name one owner more than 2 times; in every draw one owner is named exactly 2 times by every device.
All inputs are finite; a program needn't handle non-finite values.
Results may differ from a plain program's by a relative error of at most 0.009.
Values may be sent and summed in bfloat16 or wider, within the bound.
A program may use at most 128 MiB of HBM per device.

v0:
```python
import math

import jax
import jax.numpy as jnp
from jax import lax
from jax.sharding import PartitionSpec as P

D = 3200
HEADS = 16
HEAD_DIM = 128


def from_everyone(x, axis):
    copies = jnp.broadcast_to(x, (lax.axis_size(axis), *x.shape))
    return lax.all_to_all(copies, axis, split_axis=0, concat_axis=0, tiled=True)


def over_copies(x, axis):
    everything = from_everyone(x, axis)
    return jnp.sum(everything, axis=0)


def in_one(arrays, axis):
    ravelled, at, done = (jnp.concatenate([a.reshape(-1) for a in arrays]), 0, [])
    subtotal = over_copies(ravelled, axis)
    for a in arrays:
        done.append(subtotal[at : at + a.size].reshape(a.shape))
        at += a.size
    return tuple(done)


def merge_layout(grid, token_count, slot_count):
    half_rows = grid[:, 0]
    half_cols = grid[:, 1]
    image_slots = half_rows * half_cols
    slot_ends = jnp.cumsum(image_slots)
    slot_starts = slot_ends - image_slots
    slot_ids = jnp.arange(slot_count, dtype=jnp.int32)
    image_ids = jnp.sum((slot_ids[:, None] >= slot_ends[None, :]).astype(jnp.int32), axis=1)
    image_count = grid.shape[0]
    is_live = image_ids < image_count
    one_hot = (image_ids[:, None] == jnp.arange(image_count, dtype=jnp.int32)[None, :]).astype(
        jnp.int32
    )
    cols_here = jnp.maximum(jnp.sum(one_hot * half_cols[None, :], axis=1), 1)
    start_here = jnp.sum(one_hot * slot_starts[None, :], axis=1)
    offset = slot_ids - start_here
    row_half = offset // cols_here
    col_half = offset % cols_here
    first_row = 4 * start_here + 4 * row_half * cols_here + 2 * col_half
    patch_rows = jnp.stack(
        [first_row, first_row + 1, first_row + 2 * cols_here, first_row + 2 * cols_here + 1], axis=1
    )
    patch_rows = jnp.where(is_live[:, None], patch_rows, 0)
    token_ids = jnp.arange(token_count, dtype=jnp.int32)
    segment = jnp.sum((token_ids[:, None] >= 4 * slot_ends[None, :]).astype(jnp.int32), axis=1)
    return (patch_rows, is_live, segment)


def owner_ranks(owner_ids, is_live):
    slot_ids = jnp.arange(owner_ids.shape[0], dtype=jnp.int32)
    earlier = (
        (owner_ids[:, None] == owner_ids[None, :])
        & (slot_ids[None, :] < slot_ids[:, None])
        & is_live[None, :]
    )
    return jnp.sum(earlier.astype(jnp.int32), axis=1)


def body(tokens, norm_gain, w_qkv, q_gain, k_gain, w_out, grids, owners, proj_gain, proj_bias):
    token_count = tokens.shape[0]
    slot_count = owners.shape[0]
    quarter = proj_gain.shape[1]
    head_share = q_gain.shape[0]
    head_count = head_share // HEAD_DIM
    head_width = HEADS * HEAD_DIM
    score_scale = 1.0 / math.sqrt(HEAD_DIM)
    feature_total = 4 * D
    devices_req = lax.axis_size("req")
    capacity = max(2, (2 * slot_count + devices_req - 1) // devices_req)
    patch_rows, is_live, segment = merge_layout(grids, token_count, slot_count)
    token_float = tokens.astype(jnp.float32)
    mean_square = jnp.mean(token_float * token_float, axis=1, keepdims=True)
    normed = (token_float * lax.rsqrt(mean_square + 1e-06) * norm_gain).astype(jnp.bfloat16)
    projected = jnp.dot(
        normed, lax.all_gather(w_qkv, "req", axis=0, tiled=True), preferred_element_type=jnp.float32
    )
    projected = projected.reshape(token_count, head_count, 3, HEAD_DIM)
    queries = projected[:, :, 0]
    key_vecs = projected[:, :, 1]
    values = projected[:, :, 2].astype(jnp.bfloat16)
    q_gains = q_gain.reshape(head_count, HEAD_DIM)
    k_gains = k_gain.reshape(head_count, HEAD_DIM)
    local_q = jnp.sum(queries * queries, axis=(1, 2))
    local_k = jnp.sum(key_vecs * key_vecs, axis=(1, 2))
    q_total, k_total = in_one((local_q, local_k), "tp")
    q_scale = lax.rsqrt(q_total / head_width + 1e-06)
    k_scale = lax.rsqrt(k_total / head_width + 1e-06)
    q_normed = queries * q_scale[:, None, None] * q_gains
    k_normed = key_vecs * k_scale[:, None, None] * k_gains
    scores = (
        jnp.einsum("qhd,khd->hqk", q_normed, k_normed, precision=lax.Precision.HIGHEST)
        * score_scale
    )
    same_image = segment[:, None] == segment[None, :]
    scores = jnp.where(same_image[None], scores, -1e30)
    row_top = jnp.max(scores, axis=2, keepdims=True)
    weights_raw = jnp.exp(scores - row_top)
    probs = (weights_raw / jnp.sum(weights_raw, axis=2, keepdims=True)).astype(jnp.bfloat16)
    attended = jnp.einsum("hqk,khd->qhd", probs, values, preferred_element_type=jnp.float32)
    attended = attended.astype(jnp.bfloat16).reshape(token_count, head_share)
    partial_sum = jnp.dot(
        attended,
        lax.all_gather(w_out, "req", axis=1, tiled=True),
        preferred_element_type=jnp.float32,
    )
    mine = lax.psum_scatter(
        partial_sum.astype(jnp.bfloat16), "tp", scatter_dimension=1, tiled=True
    ).astype(jnp.float32)
    token_mine = lax.dynamic_slice_in_dim(token_float, lax.axis_index("tp") * quarter, quarter, 1)
    hidden = (token_mine + mine).astype(jnp.bfloat16)
    merged = jnp.where(is_live[:, None, None], hidden[patch_rows], jnp.zeros((), jnp.bfloat16))
    ranks = owner_ranks(owners, is_live)
    target_owner = jnp.where(is_live, owners, devices_req)
    merged_float = merged.astype(jnp.float32)
    row_sum = jnp.sum(merged_float, axis=(1, 2))
    row_sq = jnp.sum(merged_float * merged_float, axis=(1, 2))
    row_sum, row_sq = in_one((row_sum, row_sq), "tp")
    mean_value = row_sum / feature_total
    variance = row_sq / feature_total - mean_value * mean_value
    normed_rows = (merged_float - mean_value[:, None, None]) * lax.rsqrt(variance + 1e-05)[
        :, None, None
    ] * proj_gain + proj_bias
    normed_rows = jnp.where(is_live[:, None, None], normed_rows, 0.0).astype(jnp.bfloat16)
    send_slots = jnp.zeros((devices_req, capacity, 4, quarter), jnp.bfloat16)
    send_slots = send_slots.at[target_owner, ranks].set(normed_rows, mode="drop")
    arrived = lax.all_to_all(send_slots, "req", split_axis=0, concat_axis=0, tiled=True)
    result = arrived.reshape(devices_req * capacity, 4, quarter)
    return result


def solution(mesh):
    placed = (
        P("req", None),
        P(),
        P("req", "tp"),
        P("tp"),
        P("tp"),
        P("tp", "req"),
        P("req", None),
        P("req"),
        P(None, "tp"),
        P(None, "tp"),
    )
    return jax.shard_map(
        body, mesh=mesh, in_specs=placed, out_specs=P("req", None, "tp"), check_vma=False
    )
```

profile of v0, /device:TPU:1, one launch (start us, length us, event | category | flops | bytes accessed | tf_op | source)
XLA Modules:
  0.0 338.9 jit_solution(6515635948324033190)
XLA Ops:
  6.5 0.7 all-gather.5.cloned.1.call-update
  7.3 0.7 all-gather.7.cloned.1.call-update
  8.0 4.2 %copy.44 = bf16[384,3200]{0,1:T(8,128)(2,1)S(1)} copy(bf16[384,3200]{1,0:T(8,128)(2,1)} %param.10) | data formatting | bytes 4915200 | tf_op args[0]
  12.3 0.2 reduce-window.7
  12.5 0.6 multiply_reduce_fusion
  13.2 94.7 %all-gather.5.cloned.1.call-done = bf16[128,25,1536]{2,1,0:T(8,128)(2,1)} async-done(((bf16[1,25,1536]{2,1,0:T(8,128)(2,1)}), bf16[128,25,1536]{2,1,0:T(8,128)(2,1)}) %all-gather.5.cloned.1.call-update) | async-done | bytes 9830416 | tf_op jit(solution)/shard_map/all_gather | solution.py:86
  107.9 14.4 %reshape.394 = bf16[3200,1536]{1,0:T(8,128)(2,1)} reshape(bf16[128,25,1536]{2,1,0:T(8,128)(2,1)} %all-gather.5.cloned.1.call-done) | data formatting | bytes 19660800
  122.3 8.4 %fusion.1 = f32[384,1536]{0,1:T(8,128)S(1)} fusion(bf16[3200,1536]{1,0:T(8,128)(2,1)} %reshape.394, f32[3200]{0:T(1024)S(1)} %copy-done.8, f32[384]{0:T(512)S(1)} %add_rsqrt_fusion.2, bf16[384,3200]{0,1:T(8,128)(2,1)S(1)} %copy.44), kind=kOutput, calls=%fused_computation.6 | convolution fusion | flops 3779788800 | bytes 14661632 | tf_op jit(solution)/shard_map/dot_general | solution.py:85
  130.7 1.4 copy-done
  132.3 0.6 broadcast_in_dim.61
  132.9 4.0 %all-to-all-start = ((f32[4,1,768]{2,1,0:T(1,128)}), f32[4,1,768]{2,1,0:T(1,128)S(1)}, u32[]{:S(2)}, u32[]{:S(2)}) async-start(f32[4,1,768]{2,1,0:T(1,128)} %broadcast_in_dim.61), calls=%async_computation | async-start | bytes 24576 | tf_op jit(solution)/shard_map/all_to_all | solution.py:15
  137.1 55.0 %all-gather.7.cloned.1.call-done = bf16[128,25,512]{2,1,0:T(8,128)(2,1)} async-done(((bf16[1,25,512]{2,1,0:T(8,128)(2,1)}), bf16[128,25,512]{2,1,0:T(8,128)(2,1)}) %all-gather.7.cloned.1.call-update) | async-done | bytes 3276816 | tf_op jit(solution)/shard_map/all_gather | solution.py:114
  192.1 5.8 %reshape.396 = bf16[3200,512]{1,0:T(8,128)(2,1)} reshape(bf16[128,25,512]{2,1,0:T(8,128)(2,1)} %all-gather.7.cloned.1.call-done) | data formatting | bytes 6553600
  198.0 3.7 %fusion.15 = f32[4,384,384]{1,2,0:T(8,128)S(1)} fusion(f32[384,4,3,128]{0,3,2,1:T(8,128)} %bitcast.115, f32[4,128]{1,0:T(4,128)S(1)} %bitcast.119, f32[384]{0:T(512)S(1)} %get-tuple-element.13, f32[4,128]{1,0:T(4,128)S(1)} %bitcast.120, f32[384]{0:T(512)S(1)} %get-tuple-element.12), kind=kOutput, calls=%fused_computation.31 | convolution fusion | flops 906756096 | bytes 3939328 | tf_op jit(solution)/shard_map/qhd,khd->hqk/dot_general | solution.py:102
  201.6 1.4 copy-done.1
  203.0 0.8 fusion.44
  203.8 2.9 convolution_convert_fusion.1
  206.7 5.3 %convolution_convert_fusion = bf16[384,3200]{0,1:T(8,128)(2,1)} fusion(bf16[3200,512]{1,0:T(8,128)(2,1)} %reshape.396, bf16[384,512]{0,1:T(8,128)(2,1)S(1)} %bitcast.122), kind=kOutput, calls=%fused_computation.3 | convolution fusion | flops 1259520000 | bytes 6127616 | tf_op jit(solution)/shard_map/dot_general | solution.py:112
  212.0 2.5 convert_element_type.46
  215.3 31.2 %reduce-scatter.2.cloned.1.call-done = bf16[384,800]{0,1:T(8,128)(2,1)} async-done(((bf16[384,3200]{0,1:T(8,128)(2,1)}), bf16[384,800]{0,1:T(8,128)(2,1)}) %reduce-scatter.2.cloned.1.call-update) | async-done | bytes 614416 | tf_op jit(solution)/shard_map/reduce_scatter | solution.py:117
  246.4 1.6 add_convert_fusion
  248.0 0.3 copy.52
  248.4 2.3 gather_fusion
  250.9 1.7 convert_reduce_fusion
  252.6 0.6 broadcast_in_dim.104
  253.2 3.2 all-to-all-start.1
  256.5 4.1 %all-to-all-done.1 = f32[4,1,192]{2,1,0:T(1,128)S(1)} async-done(((f32[4,1,192]{2,1,0:T(1,128)}), f32[4,1,192]{2,1,0:T(1,128)S(1)}, u32[]{:S(2)}, u32[]{:S(2)}) %all-to-all-start.1) | async-done | bytes 3104 | tf_op jit(solution)/shard_map/all_to_all | solution.py:15
  260.7 0.7 fusion.11
  261.4 0.5 broadcast_in_dim.56
  261.9 4.6 %scatter_fusion = bf16[128,2,4,800]{3,2,1,0:T(4,128)(2,1)S(1)} fusion(bf16[128,2,4,800]{3,2,1,0:T(4,128)(2,1)S(1)} %broadcast_in_dim.56, s32[96]{0:T(128)S(1)} %fusion.34, bf16[96,4,800]{2,1,0:T(4,128)(2,1)S(1)} %fusion.11), kind=kCustom, calls=%fused_computation.1 | custom fusion | bytes 1843968 | tf_op jit(solution)/shard_map/scatter | solution.py:136
  266.5 61.8 %all_to_all.17 = bf16[128,2,4,800]{3,2,1,0:T(4,128)(2,1)} all-to-all(bf16[128,2,4,800]{3,2,1,0:T(4,128)(2,1)S(1)} %scatter_fusion), channel_id=1, replica_groups=mesh['req'=128,'tp'=4] {'req'}, dimensions={0} | all-to-all | bytes 3276800 | tf_op jit(solution)/shard_map/all_to_all | solution.py:137
  328.3 4.0 %copy.54 = bf16[256,4,800]{0,2,1:T(8,128)(2,1)} copy(bf16[256,4,800]{2,1,0:T(4,128)(2,1)} %bitcast.113) | data formatting | bytes 3276800 | tf_op jit(solution)/shard_map/reshape | solution.py:138
  (44 shorter events, 1.6 us)
Async XLA Ops:
  6.5 101.4 %all-gather.5.cloned.1.call-start = ((), (), s32[]{:S(2)}) async-start(), calls=%async_computation.5 | async-start | bytes 12681216 | tf_op jit(solution)/shard_map/all_gather | solution.py:86
  7.3 184.8 %all-gather.7.cloned.1.call-start = ((), (), s32[]{:S(2)}) async-start(), calls=%async_computation.6 | async-start | bytes 4227072 | tf_op jit(solution)/shard_map/all_gather | solution.py:114
  8.0 4.2 %copy-start.5 = (s32[3,2]{0,1:T(2,128)S(1)}, s32[3,2]{0,1:T(2,128)}, u32[]{:S(2)}) copy-start(s32[3,2]{0,1:T(2,128)} %param.16) | copy-start | bytes 76
  13.2 109.1 %copy-start.8 = (f32[3200]{0:T(1024)S(1)}, f32[3200]{0:T(1024)}, u32[]{:S(2)}) copy-start(f32[3200]{0:T(1024)} %param.11) | copy-start | bytes 38404
  130.7 1.5 copy-start
  132.9 65.0 %all-to-all-start = ((f32[4,1,768]{2,1,0:T(1,128)}), f32[4,1,768]{2,1,0:T(1,128)S(1)}, u32[]{:S(2)}, u32[]{:S(2)}) async-start(f32[4,1,768]{2,1,0:T(1,128)} %broadcast_in_dim.61), calls=%async_computation | async-start | bytes 24576 | tf_op jit(solution)/shard_map/all_to_all | solution.py:15
  136.9 109.5 %reduce-scatter.2.cloned.1.call-start = ((), (), s32[]{:S(2)}) async-start(), calls=%async_computation.4 | async-start | bytes 3072000 | tf_op jit(solution)/shard_map/reduce_scatter | solution.py:117
  137.1 60.9 %copy-start.6 = (f32[512]{0:T(512)S(1)}, f32[512]{0:T(512)}, u32[]{:S(2)}) copy-start(f32[512]{0:T(512)} %param.14) | copy-start | bytes 6148
  137.1 60.9 %copy-start.7 = (f32[512]{0:T(512)S(1)}, f32[512]{0:T(512)}, u32[]{:S(2)}) copy-start(f32[512]{0:T(512)} %param.13) | copy-start | bytes 6148
  201.6 1.4 copy-start.1
  212.0 3.1 copy-start.4
  250.7 10.0 %copy-start.2 = (f32[4,800]{1,0:T(4,128)S(1)}, f32[4,800]{1,0:T(4,128)}, u32[]{:S(2)}) copy-start(f32[4,800]{1,0:T(4,128)} %param.19) | copy-start | bytes 38404
  250.7 10.0 %copy-start.3 = (f32[4,800]{1,0:T(4,128)S(1)}, f32[4,800]{1,0:T(4,128)}, u32[]{:S(2)}) copy-start(f32[4,800]{1,0:T(4,128)} %param.18) | copy-start | bytes 38404
  253.2 7.4 %all-to-all-start.1 = ((f32[4,1,192]{2,1,0:T(1,128)}), f32[4,1,192]{2,1,0:T(1,128)S(1)}, u32[]{:S(2)}, u32[]{:S(2)}) async-start(f32[4,1,192]{2,1,0:T(1,128)} %broadcast_in_dim.104), calls=%async_computation.2 | async-start | bytes 8192 | tf_op jit(solution)/shard_map/all_to_all | solution.py:15
Sparse Core Ops, SparseCore 0:
  10.5 97.3 all-gather.4
  111.0 81.0 all-gather.6
  212.1 34.2 reduce-scatter.1
where the time goes:
time: 341 us; the launch traced here: 339 us
  waiting for transfers between devices  186 us (55%)
  blocking collectives  61.8 us (18%)
  local copies, waits for them, and re-layouts  40.6 us (12%)
  matrix products  20.3 us (6%)
  between operations  13.4 us (4%)
  other arithmetic  9.19 us (3%)
  starting transfers between devices  7.26 us (2%)
    all_gather x1, waiting for transfers between devices, body(): lax.all_gather(w_qkv, 'req', axis=0, tiled=True)  94.7 us
    all_to_all x1, blocking collectives, body(): lax.all_to_all(send_slots, 'req', split_axis=0, concat_axis=0, tiled=True)  61.8 us
    all_gather x1, waiting for transfers between devices, body(): lax.all_gather(w_out, 'req', axis=1, tiled=True)  55 us
    reduce_scatter x1, waiting for transfers between devices, body(): lax.psum_scatter(partial_sum.astype(jnp.bfloat16), 'tp', scatter_dimensio...  31.2 us
    unnamed x21, local copies, waits for them, and re-layouts  27.3 us
    dot_general x1, matrix products, body(): jnp.dot(normed, lax.all_gather(w_qkv, 'req', axis=0, tiled=True), preferr...  8.44 us
    all_to_all x2, starting transfers between devices, from_everyone(): return lax.all_to_all(copies, axis, split_axis=0, concat_axis=0, tiled=True)  7.22 us
  transfers between devices with their start and end apart: 5, of which 4 were waited for; matrix products, arithmetic and copies ran while one was open for 11% of the time, Pallas kernels for 0%

commit v1 on v0

--- a/solution.py
+++ b/solution.py
@@ -1,13 +1,21 @@
+import functools
 import math
 
 import jax
 import jax.numpy as jnp
 from jax import lax
+from jax.experimental import pallas as pl
+from jax.experimental.pallas import tpu as pltpu
 from jax.sharding import PartitionSpec as P
 
 D = 3200
 HEADS = 16
 HEAD_DIM = 128
+MESH = pl.DeviceIdType.MESH
+SIDE = 8
+SLAB = 400
+PART = ((0, 200), (200, 200))
+HALF = 104
 
 
 def from_everyone(x, axis):
@@ -65,6 +73,188 @@
         & is_live[None, :]
     )
     return jnp.sum(earlier.astype(jnp.int32), axis=1)
+
+
+def shard_of(z, y, core):
+    return (z * SIDE + y) * 2 + core
+
+
+def gather_kernel(mine, out, own_sem, send_sem, pair_sem, r1, r2):
+    me = lax.axis_index("req")
+    z = me // (2 * SIDE)
+    y = (me // 2) % SIDE
+    core = me % 2
+    partner = shard_of(z, y, 1 - core)
+
+    def up(v, by):
+        return lax.rem(v + by + SIDE, SIDE)
+
+    def ident(part, p, q):
+        return shard_of(p, q, core) if part == 0 else shard_of(q, p, core)
+
+    where = ((z, y), (y, z))
+    around = [shard_of(up(z, 1), y, core), shard_of(up(z, -1), y, core)]
+    across = [shard_of(z, up(y, 1), core), shard_of(z, up(y, -1), core)]
+    first = (around, across)
+    second = (across, around)
+
+    barrier = pltpu.get_barrier_semaphore()
+    for other in around + across + [partner]:
+        pl.semaphore_signal(barrier, inc=1, device_id={"req": other}, device_id_type=MESH)
+    pl.semaphore_wait(barrier, 5)
+
+    own = pltpu.make_async_copy(mine, out.at[me], own_sem)
+    own.start()
+
+    def piece(part, half):
+        low, rows = PART[part]
+        if half is None:
+            return low, rows
+        return (low, HALF) if half == 0 else (low + HALF, rows - HALF)
+
+    def copy(shard, part, half, sem, to, source=None):
+        low, rows = piece(part, half)
+        dst = out.at[shard, pl.ds(low, rows)]
+        src = dst if source is None else source.at[pl.ds(low, rows)]
+        return pltpu.make_async_remote_copy(
+            src_ref=src,
+            dst_ref=dst,
+            send_sem=send_sem,
+            recv_sem=sem,
+            device_id={"req": to},
+            device_id_type=MESH,
+        )
+
+    def spread(part, j, shard, source=None):
+        for way in range(2):
+            copy(shard, part, None, r2.at[part, way, 0, j], second[part][way], source).start()
+        copy(shard, part, None, pair_sem, partner, source).start()
+
+    for part in range(2):
+        for way in range(2):
+            copy(me, part, None, r1.at[part, way, 0], first[part][way], mine).start()
+    for part in range(2):
+        spread(part, 0, me, mine)
+    for k in range(1, 5):
+        for part in range(2):
+            p, q = where[part]
+            if k < 4:
+                for way in range(2):
+                    shard = ident(part, up(p, -k if way == 0 else k), q)
+                    copy(shard, part, None, r1.at[part, way, k - 1], partner).wait_recv()
+                    half = None if k < 3 else way
+                    copy(shard, part, half, r1.at[part, way, k], first[part][way]).start()
+                    spread(part, 2 * k - 1 + way, shard)
+            else:
+                shard = ident(part, up(p, 4), q)
+                for way in range(2):
+                    copy(shard, part, way, r1.at[part, way, 3], partner).wait_recv()
+                spread(part, 7, shard)
+    for h in range(1, 5):
+
+        def step(j, carry):
+            sign = 1 - 2 * (j % 2)
+            off = ((j + 1) // 2) * sign
+            for part in range(2):
+                p, q = where[part]
+                p_here = up(p, off)
+                if h < 4:
+                    for way in range(2):
+                        shard = ident(part, p_here, up(q, -h if way == 0 else h))
+                        copy(shard, part, None, r2.at[part, way, h - 1, j], partner).wait_recv()
+                        half = None if h < 3 else way
+                        copy(shard, part, half, r2.at[part, way, h, j], second[part][way]).start()
+                        copy(shard, part, None, pair_sem, partner).start()
+                else:
+                    shard = ident(part, p_here, up(q, 4))
+                    for way in range(2):
+                        copy(shard, part, way, r2.at[part, way, 3, j], partner).wait_recv()
+                    copy(shard, part, None, pair_sem, partner).start()
+            return carry
+
+        lax.fori_loop(0, SIDE, step, 0)
+
+    own.wait()
+    half_all = out.at[pl.ds(0, 64)]
+    pltpu.make_async_copy(half_all, half_all, pair_sem).wait()
+    sent = out.at[pl.ds(0, 127)]
+    pltpu.make_async_copy(sent, sent, send_sem).wait()
+
+
+def gather_weights(slab):
+    count = lax.axis_size("req")
+    return pl.pallas_call(
+        gather_kernel,
+        out_shape=jax.ShapeDtypeStruct((count, SLAB, 128), jnp.bfloat16),
+        in_specs=[pl.BlockSpec(memory_space=pl.ANY)],
+        out_specs=pl.BlockSpec(memory_space=pl.ANY),
+        scratch_shapes=[
+            pltpu.SemaphoreType.DMA,
+            pltpu.SemaphoreType.DMA,
+            pltpu.SemaphoreType.DMA,
+            pltpu.SemaphoreType.DMA((2, 2, 4)),
+            pltpu.SemaphoreType.DMA((2, 2, 4, SIDE)),
+        ],
+        compiler_params=pltpu.CompilerParams(collective_id=0, has_side_effects=True),
+        name="gather_weights",
+    )(slab)
+
+
+def norm_kernel(tokens, gain, out, normed):
+    x = tokens[...].astype(jnp.float32)
+    square = jnp.mean(x * x, axis=1, keepdims=True)
+    normed[...] = (x * lax.rsqrt(square + 1e-06) * gain[...]).astype(jnp.bfloat16)
+    for j in range(24):
+        start = (128 * j + (128 * j) // 24) // 128 * 128
+        width = min(384, D - start)
+        source = lax.broadcasted_iota(jnp.int32, (width, 128), 0) + start
+        target = lax.broadcasted_iota(jnp.int32, (width, 128), 1) + 128 * j
+        pick = (source == target + target // 24).astype(jnp.bfloat16)
+        out[:, 128 * j : 128 * (j + 1)] = jnp.dot(
+            normed[:, start : start + width], pick, preferred_element_type=jnp.float32
+        ).astype(jnp.bfloat16)
+    source = lax.broadcasted_iota(jnp.int32, (D, 128), 0)
+    target = lax.broadcasted_iota(jnp.int32, (D, 128), 1)
+    pick = (source == target * 25 + 24).astype(jnp.bfloat16)
+    out[:, 3072:] = jnp.dot(normed[...], pick, preferred_element_type=jnp.float32).astype(
+        jnp.bfloat16
+    )
+
+
+def norm_tokens(tokens, gain):
+    return pl.pallas_call(
+        norm_kernel,
+        out_shape=jax.ShapeDtypeStruct(tokens.shape, jnp.bfloat16),
+        scratch_shapes=[pltpu.VMEM(tokens.shape, jnp.bfloat16)],
+        compiler_params=pltpu.CompilerParams(vmem_limit_bytes=60 << 20),
+        name="norm_tokens",
+    )(tokens, gain.reshape(1, D))
+
+
+def project_kernel(x, blocks, left, out):
+    weight = jnp.concatenate(
+        [blocks[:, :24].reshape(3072, 128), blocks[:, 24:].reshape(3072, 128)], axis=1
+    )
+    total = jnp.dot(x[:, :3072], weight, preferred_element_type=jnp.float32)
+    total += jnp.dot(x[:, 3072:], left[...], preferred_element_type=jnp.float32)
+    out[...] = total
+
+
+def project(x, gathered, left):
+    rows = x.shape[0]
+    return pl.pallas_call(
+        project_kernel,
+        grid=(6,),
+        out_shape=jax.ShapeDtypeStruct((rows, 1536), jnp.float32),
+        in_specs=[
+            pl.BlockSpec((rows, D), lambda i: (0, 0)),
+            pl.BlockSpec((128, 48, 128), lambda i: (0, i, 0)),
+            pl.BlockSpec((128, 256), lambda i: (0, i)),
+        ],
+        out_specs=pl.BlockSpec((rows, 256), lambda i: (0, i)),
+        compiler_params=pltpu.CompilerParams(vmem_limit_bytes=60 << 20),
+        name="project",
+    )(x, gathered, left)
 
 
 def body(tokens, norm_gain, w_qkv, q_gain, k_gain, w_out, grids, owners, proj_gain, proj_bias):
@@ -80,11 +270,23 @@
     capacity = max(2, (2 * slot_count + devices_req - 1) // devices_req)
     patch_rows, is_live, segment = merge_layout(grids, token_count, slot_count)
     token_float = tokens.astype(jnp.float32)
-    mean_square = jnp.mean(token_float * token_float, axis=1, keepdims=True)
-    normed = (token_float * lax.rsqrt(mean_square + 1e-06) * norm_gain).astype(jnp.bfloat16)
-    projected = jnp.dot(
-        normed, lax.all_gather(w_qkv, "req", axis=0, tiled=True), preferred_element_type=jnp.float32
-    )
+
+    both = jnp.concatenate([w_qkv, w_out.T], axis=1)
+    slab = jnp.concatenate(
+        [
+            both[:24].reshape(24, 16, 128).transpose(1, 0, 2).reshape(384, 128),
+            both[24].reshape(16, 128),
+        ],
+        axis=0,
+    )
+    gathered = gather_weights(slab)
+    normed = norm_tokens(tokens, norm_gain)
+    left = gathered[:, 384:, :].reshape(devices_req, 2048)
+    projected = project(normed, gathered, left[:, :1536])
+    out_rows = gathered[:, 288:384, :].reshape(devices_req, 4, 24, 128)
+    out_left = gathered[:, 396:400, :].reshape(devices_req, 4, 1, 128)
+    w_out_all = jnp.concatenate([out_rows, out_left], axis=2)
+
     projected = projected.reshape(token_count, head_count, 3, HEAD_DIM)
     queries = projected[:, :, 0]
     key_vecs = projected[:, :, 1]
@@ -108,12 +310,10 @@
     weights_raw = jnp.exp(scores - row_top)
     probs = (weights_raw / jnp.sum(weights_raw, axis=2, keepdims=True)).astype(jnp.bfloat16)
     attended = jnp.einsum("hqk,khd->qhd", probs, values, preferred_element_type=jnp.float32)
-    attended = attended.astype(jnp.bfloat16).reshape(token_count, head_share)
-    partial_sum = jnp.dot(
-        attended,
-        lax.all_gather(w_out, "req", axis=1, tiled=True),
-        preferred_element_type=jnp.float32,
-    )
+    attended = attended.astype(jnp.bfloat16)
+    partial_sum = jnp.einsum(
+        "qhd,shrd->qsr", attended, w_out_all, preferred_element_type=jnp.float32
+    ).reshape(token_count, D)
     mine = lax.psum_scatter(
         partial_sum.astype(jnp.bfloat16), "tp", scatter_dimension=1, tiled=True
     ).astype(jnp.float32)

time: 341 us -> 245 us (0.72)
  waiting for transfers between devices: 186 us -> 37.6 us
  Pallas kernels: 0 us -> 73.3 us
  matrix products: 20.3 us -> 9.08 us
  local copies, waits for them, and re-layouts: 40.6 us -> 32.7 us
    all_gather x2 -> x0, waiting for transfers between devices: 150 us -> none  [the longest x1 94.7 us: body(): lax.all_gather(w_qkv, 'req', axis=0, tiled=True)]
    pallas_call x0 -> x3, Pallas kernels: none -> 73.3 us  [the longest x1 57.2 us: gather_weights(): pl.pallas_call(gather_kernel, out_shape=jax.ShapeDtypeStruct((count, SLAB...]
    unnamed x3 -> x2, waiting for transfers between devices: 1.42 us -> 33.5 us
    reduce_scatter x1 -> x0, waiting for transfers between devices: 31.2 us -> none  [body(): lax.psum_scatter(partial_sum.astype(jnp.bfloat16), 'tp', scatter_dimensio...]
    unnamed x21 -> x16, local copies, waits for them, and re-layouts: 27.3 us -> 3.01 us
    dot_general x3 -> x1, matrix products: 16.6 us -> 6.79 us  [body(): jnp.einsum('qhd,shrd->qsr', attended, w_out_all, preferred_element_type=j...]
    convert_element_type x1 -> x2, local copies, waits for them, and re-layouts: 0.35 us -> 5.75 us  [body(): partial_sum.astype(jnp.bfloat16)]
    reshape x0 -> x4, local copies, waits for them, and re-layouts: none -> 5.24 us  [the longest x1 2.88 us: body(): out_rows = gathered[:, 288:384, :].reshape(devices_req, 4, 24, 128)]
  transfers between devices with their start and end apart: 5 -> 3, of which waited for: 4 -> 2; matrix products, arithmetic and copies ran while one was open for 11% -> 2% of each run, Pallas kernels for 0% -> 0%
where the time goes in v1:
time: 245 us; the launch traced here: 244 us
  Pallas kernels  73.3 us (30%)
  blocking collectives  61.8 us (25%)
  waiting for transfers between devices  37.6 us (15%)
  local copies, waits for them, and re-layouts  32.7 us (13%)
  between operations  13.6 us (6%)
  matrix products  9.08 us (4%)
  other arithmetic  8.31 us (3%)
  starting transfers between devices  7.26 us (3%)
    all_to_all x1, blocking collectives, body(): lax.all_to_all(send_slots, 'req', split_axis=0, concat_axis=0, tiled=True)  61.8 us
    pallas_call x1, Pallas kernels, gather_weights(): pl.pallas_call(gather_kernel, out_shape=jax.ShapeDtypeStruct((count, SLAB...  57.2 us
    unnamed x2, waiting for transfers between devices  33.5 us
    pallas_call x1, Pallas kernels, project(): pl.pallas_call(project_kernel, grid=(6,), out_shape=jax.ShapeDtypeStruct(...  9.72 us
    all_to_all x2, starting transfers between devices, from_everyone(): return lax.all_to_all(copies, axis, split_axis=0, concat_axis=0, tiled=True)  7.26 us
    dot_general x1, matrix products, body(): jnp.einsum('qhd,shrd->qsr', attended, w_out_all, preferred_element_type=j...  6.79 us
    pallas_call x1, Pallas kernels, norm_tokens(): pl.pallas_call(norm_kernel, out_shape=jax.ShapeDtypeStruct(tokens.shape,...  6.4 us
    convert_element_type x2, local copies, waits for them, and re-layouts, body(): partial_sum.astype(jnp.bfloat16)  5.75 us
  transfers between devices with their start and end apart: 3, of which 2 were waited for; matrix products, arithmetic and copies ran while one was open for 2% of the time, Pallas kernels for 0%

profile of v1, /device:TPU:1, one launch (start us, length us, event | category | flops | bytes accessed | tf_op | source)
XLA Modules:
  0.0 243.7 jit_solution(14117903863312217544)
XLA Ops:
  6.5 0.8 fusion.34
  7.3 0.9 copy_bitcast_fusion.1
  8.2 1.3 reshape.383.gain
  9.6 0.6 pad_maximum_fusion.mine
  10.2 57.2 %gather_weights.1.blocks = bf16[128,400,128]{2,1,0:T(8,128)(2,1)} custom-call(bf16[400,128]{1,0:T(8,128)(2,1)} %pad_maximum_fusion.mine), custom_call_target="tpu_custom_call" | custom-call | tf_op jit(solution)/shard_map/gather_weights/pallas_call | solution.py:186
  67.4 1.1 slice.50
  68.7 0.8 slice.67.left
  69.4 6.4 %norm_tokens.1.x = bf16[384,3200]{1,0:T(8,128)(2,1)} custom-call(bf16[384,3200]{1,0:T(8,128)(2,1)} %tokens.1, f32[1,3200]{1,0:T(1,128)} %reshape.383.gain), custom_call_target="tpu_custom_call" | custom-call | tf_op jit(solution)/shard_map/norm_tokens/pallas_call | solution.py:225
  75.8 9.7 %project.1 = f32[384,1536]{1,0:T(8,128)} custom-call(bf16[384,3200]{1,0:T(8,128)(2,1)} %norm_tokens.1.x, bf16[128,400,128]{2,1,0:T(8,128)(2,1)} %gather_weights.1.blocks, bf16[128,1536]{1,0:T(8,128)(2,1)} %slice.67.left), custom_call_target="tpu_custom_call" | custom-call | tf_op jit(solution)/shard_map/project/pallas_call | solution.py:245
  85.5 2.0 copy.56
  87.8 0.6 broadcast_in_dim.61
  88.4 4.0 %all-to-all-start = ((f32[4,1,768]{2,1,0:T(1,128)}), f32[4,1,768]{2,1,0:T(1,128)S(1)}, u32[]{:S(2)}, u32[]{:S(2)}) async-start(f32[4,1,768]{2,1,0:T(1,128)} %broadcast_in_dim.61), calls=%async_computation | async-start | bytes 24576 | tf_op jit(solution)/shard_map/all_to_all | solution.py:23
  92.4 1.0 slice_bitcast_fusion.4
  93.9 1.9 slice-done
  95.8 2.9 %copy.63 = bf16[128,4,24,128]{3,0,1,2:T(8,128)(2,1)} copy(bf16[128,4,24,128]{3,2,1,0:T(8,128)(2,1)S(1)} %bitcast.134) | data formatting | bytes 6291456 | tf_op jit(solution)/shard_map/reshape | solution.py:286
  98.7 2.3 fusion.18
  101.0 1.4 copy-done
  102.4 0.8 fusion.55
  103.2 6.8 %bitcast_convert_fusion = bf16[384,128,25]{0,1,2:T(8,128)(2,1)} fusion(bf16[128,4,1,128]{3,0,1,2:T(8,128)(2,1)S(1)} %copy.64, bf16[128,4,24,128]{3,0,1,2:T(8,128)(2,1)} %copy.63, f32[4,384]{1,0:T(4,128)S(1)} %fusion.55, f32[384,4,3,128]{0,3,2,1:T(8,128)S(1)} %bitcast.137, f32[4,384,384]{1,2,0:T(8,128)} %copy-done, pred[384,384]{0,1:T(8,128)(4,1)S(1)} %broadcast_compare_fusion), kind=kOutput, calls=%fused_computation.3 | convolution fusion | flops 1420216192 | bytes 8640512 | tf_op jit(solution)/shard_map/qhd,shrd->qsr/dot_general | solution.py:314
  109.9 3.2 %copy.66 = bf16[384,128,25]{0,2,1:T(8,128)(2,1)S(1)} copy(bf16[384,128,25]{0,1,2:T(8,128)(2,1)} %bitcast_convert_fusion) | data formatting | bytes 4915200 | tf_op jit(solution)/shard_map/convert_element_type | solution.py:318
  113.1 2.6 %convert_element_type.53 = bf16[384,3200]{0,1:T(8,128)(2,1)} reshape(bf16[384,128,25]{0,2,1:T(8,128)(2,1)S(1)} %copy.66) | data formatting | bytes 4915200 | tf_op jit(solution)/shard_map/convert_element_type | solution.py:318
  116.5 33.5 %reduce-scatter.4.cloned.1.call-done = bf16[800,384]{1,0:T(8,128)(2,1)} async-done(((bf16[3200,384]{1,0:T(8,128)(2,1)}), bf16[800,384]{1,0:T(8,128)(2,1)}) %reduce-scatter.4.cloned.1.call-update) | async-done | bytes 614416
  150.0 1.4 copy.80
  151.4 1.5 add_convert_fusion
  152.9 2.3 gather_fusion
  155.4 1.7 convert_reduce_fusion
  157.7 3.2 %all-to-all-start.1 = ((f32[4,1,192]{2,1,0:T(1,128)}), f32[4,1,192]{2,1,0:T(1,128)S(1)}, u32[]{:S(2)}, u32[]{:S(2)}) async-start(f32[4,1,192]{2,1,0:T(1,128)} %broadcast_in_dim.102), calls=%async_computation.1 | async-start | bytes 8192 | tf_op jit(solution)/shard_map/all_to_all | solution.py:23
  161.0 4.1 %all-to-all-done.1 = f32[4,1,192]{2,1,0:T(1,128)S(1)} async-done(((f32[4,1,192]{2,1,0:T(1,128)}), f32[4,1,192]{2,1,0:T(1,128)S(1)}, u32[]{:S(2)}, u32[]{:S(2)}) %all-to-all-start.1) | async-done | bytes 3104 | tf_op jit(solution)/shard_map/all_to_all | solution.py:23
  165.2 0.7 fusion.13
  166.5 4.6 %scatter_fusion = bf16[128,2,4,800]{3,2,1,0:T(4,128)(2,1)S(1)} fusion(bf16[128,2,4,800]{3,2,1,0:T(4,128)(2,1)S(1)} %broadcast_in_dim.56, s32[96]{0:T(128)S(1)} %fusion.41, bf16[96,4,800]{2,1,0:T(4,128)(2,1)S(1)} %fusion.13), kind=kCustom, calls=%fused_computation.1 | custom fusion | bytes 1843968 | tf_op jit(solution)/shard_map/scatter | solution.py:336
  171.1 61.8 %all_to_all.17 = bf16[128,2,4,800]{3,2,1,0:T(4,128)(2,1)} all-to-all(bf16[128,2,4,800]{3,2,1,0:T(4,128)(2,1)S(1)} %scatter_fusion), channel_id=1, replica_groups=mesh['req'=128,'tp'=4] {'req'}, dimensions={0} | all-to-all | bytes 3276800 | tf_op jit(solution)/shard_map/all_to_all | solution.py:337
  232.8 4.0 %copy.70 = bf16[256,4,800]{0,2,1:T(8,128)(2,1)} copy(bf16[256,4,800]{2,1,0:T(4,128)(2,1)} %bitcast.139) | data formatting | bytes 3276800 | tf_op jit(solution)/shard_map/reshape | solution.py:338
  (44 shorter events, 3.0 us)
Async XLA Ops:
  85.5 7.9 %copy-start.4 = (s32[3,2]{0,1:T(2,128)S(1)}, s32[3,2]{0,1:T(2,128)}, u32[]{:S(2)}) copy-start(s32[3,2]{0,1:T(2,128)} %param.16) | copy-start | bytes 76
  88.4 10.3 %all-to-all-start = ((f32[4,1,768]{2,1,0:T(1,128)}), f32[4,1,768]{2,1,0:T(1,128)S(1)}, u32[]{:S(2)}, u32[]{:S(2)}) async-start(f32[4,1,768]{2,1,0:T(1,128)} %broadcast_in_dim.61), calls=%async_computation | async-start | bytes 24576 | tf_op jit(solution)/shard_map/all_to_all | solution.py:23
  92.4 57.6 %reduce-scatter.4.cloned.1.call-start = ((), (), s32[]{:S(2)}) async-start(), calls=%async_computation.4 | async-start | bytes 3072000
  93.9 1.9 slice-start
  95.7 2.9 %copy-start.5 = (f32[512]{0:T(512)S(1)}, f32[512]{0:T(512)}, u32[]{:S(2)}) copy-start(f32[512]{0:T(512)} %param.14) | copy-start | bytes 6148
  95.7 2.9 %copy-start.6 = (f32[512]{0:T(512)S(1)}, f32[512]{0:T(512)}, u32[]{:S(2)}) copy-start(f32[512]{0:T(512)} %param.13) | copy-start | bytes 6148
  101.0 1.4 copy-start
  115.7 0.7 copy-start.3
  155.2 10.0 %copy-start.1 = (f32[4,800]{1,0:T(4,128)S(1)}, f32[4,800]{1,0:T(4,128)}, u32[]{:S(2)}) copy-start(f32[4,800]{1,0:T(4,128)} %param.19) | copy-start | bytes 38404
  155.2 10.0 %copy-start.2 = (f32[4,800]{1,0:T(4,128)S(1)}, f32[4,800]{1,0:T(4,128)}, u32[]{:S(2)}) copy-start(f32[4,800]{1,0:T(4,128)} %param.18) | copy-start | bytes 38404
  157.7 7.4 %all-to-all-start.1 = ((f32[4,1,192]{2,1,0:T(1,128)}), f32[4,1,192]{2,1,0:T(1,128)S(1)}, u32[]{:S(2)}, u32[]{:S(2)}) async-start(f32[4,1,192]{2,1,0:T(1,128)} %broadcast_in_dim.102), calls=%async_computation.1 | async-start | bytes 8192 | tf_op jit(solution)/shard_map/all_to_all | solution.py:23
Sparse Core Ops, SparseCore 0:
  115.8 34.1 reduce-scatter.3

commit v2 on v1

v2 whole, which is shorter than its diff:
```python
import functools
import math

import jax
import jax.numpy as jnp
from jax import lax
from jax.experimental import pallas as pl
from jax.experimental.pallas import tpu as pltpu
from jax.sharding import PartitionSpec as P

D = 3200
HEADS = 16
HEAD_DIM = 128
MESH = pl.DeviceIdType.MESH
SIDE = 8
SLAB = 400
PART = ((0, 200), (200, 200))
HALF = 104
TOK = 384
SHARE = 800


def shard_of(z, y, core):
    return (z * SIDE + y) * 2 + core


def gather_kernel(mine, out, own_sem, send_sem, pair_sem, r1, r2):
    me = lax.axis_index("req")
    z = me // (2 * SIDE)
    y = (me // 2) % SIDE
    core = me % 2
    partner = shard_of(z, y, 1 - core)

    def up(v, by):
        return lax.rem(v + by + SIDE, SIDE)

    def ident(part, p, q):
        return shard_of(p, q, core) if part == 0 else shard_of(q, p, core)

    where = ((z, y), (y, z))
    around = [shard_of(up(z, 1), y, core), shard_of(up(z, -1), y, core)]
    across = [shard_of(z, up(y, 1), core), shard_of(z, up(y, -1), core)]
    first = (around, across)
    second = (across, around)

    barrier = pltpu.get_barrier_semaphore()
    for other in around + across + [partner]:
        pl.semaphore_signal(barrier, inc=1, device_id={"req": other}, device_id_type=MESH)
    pl.semaphore_wait(barrier, 5)

    own = pltpu.make_async_copy(mine, out.at[me], own_sem)
    own.start()

    def piece(part, half):
        low, rows = PART[part]
        if half is None:
            return low, rows
        return (low, HALF) if half == 0 else (low + HALF, rows - HALF)

    def copy(shard, part, half, sem, to, source=None):
        low, rows = piece(part, half)
        dst = out.at[shard, pl.ds(low, rows)]
        src = dst if source is None else source.at[pl.ds(low, rows)]
        return pltpu.make_async_remote_copy(
            src_ref=src,
            dst_ref=dst,
            send_sem=send_sem,
            recv_sem=sem,
            device_id={"req": to},
            device_id_type=MESH,
        )

    def spread(part, j, shard, source=None):
        for way in range(2):
            copy(shard, part, None, r2.at[part, way, 0, j], second[part][way], source).start()
        copy(shard, part, None, pair_sem, partner, source).start()

    for part in range(2):
        for way in range(2):
            copy(me, part, None, r1.at[part, way, 0], first[part][way], mine).start()
    for part in range(2):
        spread(part, 0, me, mine)
    for k in range(1, 5):
        for part in range(2):
            p, q = where[part]
            if k < 4:
                for way in range(2):
                    shard = ident(part, up(p, -k if way == 0 else k), q)
                    copy(shard, part, None, r1.at[part, way, k - 1], partner).wait_recv()
                    half = None if k < 3 else way
                    copy(shard, part, half, r1.at[part, way, k], first[part][way]).start()
                    spread(part, 2 * k - 1 + way, shard)
            else:
                shard = ident(part, up(p, 4), q)
                for way in range(2):
                    copy(shard, part, way, r1.at[part, way, 3], partner).wait_recv()
                spread(part, 7, shard)
    for h in range(1, 5):

        def step(j, carry):
            sign = 1 - 2 * (j % 2)
            off = ((j + 1) // 2) * sign
            for part in range(2):
                p, q = where[part]
                p_here = up(p, off)
                if h < 4:
                    for way in range(2):
                        shard = ident(part, p_here, up(q, -h if way == 0 else h))
                        copy(shard, part, None, r2.at[part, way, h - 1, j], partner).wait_recv()
                        half = None if h < 3 else way
                        copy(shard, part, half, r2.at[part, way, h, j], second[part][way]).start()
                        copy(shard, part, None, pair_sem, partner).start()
                else:
                    shard = ident(part, p_here, up(q, 4))
                    for way in range(2):
                        copy(shard, part, way, r2.at[part, way, 3, j], partner).wait_recv()
                    copy(shard, part, None, pair_sem, partner).start()
            return carry

        lax.fori_loop(0, SIDE, step, 0)

    own.wait()
    half_all = out.at[pl.ds(0, 64)]
    pltpu.make_async_copy(half_all, half_all, pair_sem).wait()
    sent = out.at[pl.ds(0, 127)]
    pltpu.make_async_copy(sent, sent, send_sem).wait()


def gather_weights(slab):
    count = lax.axis_size("req")
    return pl.pallas_call(
        gather_kernel,
        out_shape=jax.ShapeDtypeStruct((count, SLAB, 128), jnp.bfloat16),
        in_specs=[pl.BlockSpec(memory_space=pl.ANY)],
        out_specs=pl.BlockSpec(memory_space=pl.ANY),
        scratch_shapes=[
            pltpu.SemaphoreType.DMA,
            pltpu.SemaphoreType.DMA,
            pltpu.SemaphoreType.DMA,
            pltpu.SemaphoreType.DMA((2, 2, 4)),
            pltpu.SemaphoreType.DMA((2, 2, 4, SIDE)),
        ],
        compiler_params=pltpu.CompilerParams(collective_id=0, has_side_effects=True),
        name="gather_weights",
    )(slab)


def norm_kernel(tokens, gain, out, token_share, normed):
    x = tokens[...].astype(jnp.float32)
    square = jnp.mean(x * x, axis=1, keepdims=True)
    normed[...] = (x * lax.rsqrt(square + 1e-06) * gain[...]).astype(jnp.bfloat16)
    for j in range(24):
        start = (128 * j + (128 * j) // 24) // 128 * 128
        width = min(384, D - start)
        source = lax.broadcasted_iota(jnp.int32, (width, 128), 0) + start
        target = lax.broadcasted_iota(jnp.int32, (width, 128), 1) + 128 * j
        pick = (source == target + target // 24).astype(jnp.bfloat16)
        out[:, 128 * j : 128 * (j + 1)] = jnp.dot(
            normed[:, start : start + width], pick, preferred_element_type=jnp.float32
        ).astype(jnp.bfloat16)
    source = lax.broadcasted_iota(jnp.int32, (D, 128), 0)
    target = lax.broadcasted_iota(jnp.int32, (D, 128), 1)
    pick = (source == target * 25 + 24).astype(jnp.bfloat16)
    out[:, 3072:] = jnp.dot(normed[...], pick, preferred_element_type=jnp.float32).astype(
        jnp.bfloat16
    )
    tp = lax.axis_index("tp")
    window = tokens[:, pl.ds(pl.multiple_of(tp * 768, 128), 896)]
    row = lax.broadcasted_iota(jnp.int32, (SHARE, 896), 0)
    lane = lax.broadcasted_iota(jnp.int32, (SHARE, 896), 1)
    feature = jnp.where(row < 768, row + row // 24, (row - 768) * 25 + 24)
    pick = (lane == feature + 32 * tp).astype(jnp.bfloat16)
    token_share[...] = lax.dot_general(
        pick, window, (((1,), (1,)), ((), ())), preferred_element_type=jnp.float32
    ).astype(jnp.bfloat16)


def norm_tokens(tokens, gain):
    return pl.pallas_call(
        norm_kernel,
        out_shape=(
            jax.ShapeDtypeStruct(tokens.shape, jnp.bfloat16),
            jax.ShapeDtypeStruct((SHARE, tokens.shape[0]), jnp.bfloat16),
        ),
        scratch_shapes=[pltpu.VMEM(tokens.shape, jnp.bfloat16)],
        compiler_params=pltpu.CompilerParams(vmem_limit_bytes=60 << 20),
        name="norm_tokens",
    )(tokens, gain.reshape(1, D))


def as_column(row):
    n = row.shape[1]
    return jnp.transpose(jnp.broadcast_to(row, (128, n)))[:, :1]


def finish_kernel(
    x_ref, token_share, left, q_gain, k_gain, grids, owners, p_gain, p_bias, gathered,
    out,
    wq, wo_raw, wo, proj, v_t, att, own_part, hold, sums, relay_in, final_in, hidden,
    stat_mine, stat_in, row_mine, row_in, slots,
    load_sem, stat_sem, row_sem, relay_sem, final_sem, send_sem, out_sem, own_sem,
):
    me = lax.axis_index("req")
    tp = lax.axis_index("tp")
    z = me // (2 * SIDE)
    devices = lax.axis_size("req")
    right = lax.rem(tp + 1, 4)
    opposite = lax.rem(tp + 2, 4)
    left_x = lax.rem(tp + 3, 4)

    barrier = pltpu.get_barrier_semaphore()

    def greet(i, carry):
        other = lax.rem(me + i, devices)
        pl.semaphore_signal(barrier, inc=1, device_id={"req": other}, device_id_type=MESH)
        return carry

    lax.fori_loop(1, devices, greet, 0)
    for other in (right, opposite, left_x):
        pl.semaphore_signal(barrier, inc=1, device_id={"tp": other}, device_id_type=MESH)

    loads = [
        pltpu.make_async_copy(gathered.at[:, pl.ds(48 * i, 48)], wq.at[i], load_sem.at[i])
        for i in range(6)
    ]
    loads.append(pltpu.make_async_copy(gathered.at[:, pl.ds(288, 96)], wo_raw, load_sem.at[6]))
    for load in loads:
        load.start()

    def project(i, carry):
        pltpu.make_async_copy(
            gathered.at[:, pl.ds(0, 48)], wq.at[i], load_sem.at[i]
        ).wait()
        weight = jnp.concatenate(
            [wq[i, :, :24].reshape(3072, 128), wq[i, :, 24:].reshape(3072, 128)], axis=1
        )
        at = pl.multiple_of(i * 256, 256)
        total = jnp.dot(x_ref[:, :3072], weight, preferred_element_type=jnp.float32)
        total += jnp.dot(
            x_ref[:, 3072:], left[:, pl.ds(at, 256)], preferred_element_type=jnp.float32
        )
        proj[:, pl.ds(at, 256)] = total
        return carry

    lax.fori_loop(0, 6, project, 0)

    pl.semaphore_wait(barrier, devices - 1 + 3)

    def to_row(other, mine, into, sem, total_sem):
        return pltpu.make_async_remote_copy(
            src_ref=mine,
            dst_ref=into.at[tp],
            send_sem=total_sem,
            recv_sem=sem,
            device_id={"tp": other},
            device_id_type=MESH,
        )

    q_sum = jnp.zeros((TOK, 1), jnp.float32)
    k_sum = jnp.zeros((TOK, 1), jnp.float32)
    for h in range(4):
        q = proj[:, h * 384 : h * 384 + 128]
        k = proj[:, h * 384 + 128 : h * 384 + 256]
        q_sum += jnp.sum(q * q, axis=1, keepdims=True)
        k_sum += jnp.sum(k * k, axis=1, keepdims=True)
    lane = lax.broadcasted_iota(jnp.int32, (TOK, 128), 1)
    both = jnp.where(lane == 0, q_sum, jnp.where(lane == 1, k_sum, 0.0))
    stat_mine[...] = jnp.transpose(both)[:8]
    stat_in[pl.ds(tp, 1)] = stat_mine[...][None]
    stat_copies = [
        to_row(o, stat_mine, stat_in, stat_sem.at[0], stat_sem.at[1])
        for o in (opposite, right, left_x)
    ]
    for c in stat_copies:
        c.start()

    for h in range(4):
        v_t[h] = jnp.transpose(proj[:, h * 384 + 256 : h * 384 + 384]).astype(jnp.bfloat16)
    loads[6].wait()

    def pack(t, carry):
        at = pl.multiple_of(t * 32, 32)
        for b in range(4):
            block = wo_raw[pl.ds(at, 32), b * 24 : (b + 1) * 24]
            wo[t, :768, b * 128 : (b + 1) * 128] = block.reshape(768, 128)
        wo[t, 768:] = left[pl.ds(at, 32), 1536:]
        return carry

    lax.fori_loop(0, 4, pack, 0)

    ends = []
    total = 0
    for i in range(3):
        total = total + grids[i, 0] * grids[i, 1]
        ends.append(total)

    def segment(ids, scale):
        found = jnp.zeros(ids.shape, jnp.int32)
        for e in ends:
            found += (ids >= scale * e).astype(jnp.int32)
        return found

    key_segment = segment(lax.broadcasted_iota(jnp.int32, (TOK, 128), 0), 4)

    pltpu.make_async_copy(stat_in.at[pl.ds(0, 3)], stat_in.at[pl.ds(0, 3)], stat_sem.at[0]).wait()
    totals = stat_in[0] + stat_in[1] + stat_in[2] + stat_in[3]
    scales = lax.rsqrt(totals / (HEADS * HEAD_DIM) + 1e-06)
    q_scale = as_column(scales[0:1])
    k_scale = as_column(scales[1:2])
    for h in range(4):
        at = h * 384
        head = slice(h * 128, (h + 1) * 128)
        proj[:, at : at + 128] = proj[:, at : at + 128] * q_scale * q_gain[:, head]
        proj[:, at + 128 : at + 256] = proj[:, at + 128 : at + 256] * k_scale * k_gain[:, head]

    def push(source, into, sem, other):
        return pltpu.make_async_remote_copy(
            src_ref=source,
            dst_ref=into,
            send_sem=send_sem.at[0],
            recv_sem=sem,
            device_id={"tp": other},
            device_id_type=MESH,
        )

    low, high = pl.ds(0, 400), pl.ds(400, 400)

    def relay(b):
        for way, (rows, other) in enumerate(((low, right), (high, left_x))):
            push(relay_in.at[way, b], relay_in.at[way, b], relay_sem.at[way, b], other).wait_recv()
            total = hold[way, b] + relay_in[way, b].astype(jnp.float32)
            sums[1 + way, b, rows] = total.astype(jnp.bfloat16)
            push(
                sums.at[1 + way, b, rows], final_in.at[way, b, rows],
                final_sem.at[way, b, 1], other,
            ).start()

    for b in range(3):
        q_at = slice(b * 128, (b + 1) * 128)
        same = key_segment == segment(
            lax.broadcasted_iota(jnp.int32, (TOK, 128), 1) + 128 * b, 4
        )
        for h in range(4):
            at = h * 384
            scores = lax.dot_general(
                proj[:, at + 128 : at + 256],
                proj[q_at, at : at + 128],
                (((1,), (1,)), ((), ())),
                precision=lax.Precision.HIGHEST,
                preferred_element_type=jnp.float32,
            ) * (1.0 / math.sqrt(HEAD_DIM))
            scores = jnp.where(same, scores, -1e30)
            raw = jnp.exp(scores - jnp.max(scores, axis=0, keepdims=True))
            probs = (raw * (1.0 / jnp.sum(raw, axis=0, keepdims=True))).astype(jnp.bfloat16)
            att[b, h * 128 : (h + 1) * 128] = jnp.dot(
                v_t[h], probs, preferred_element_type=jnp.float32
            ).astype(jnp.bfloat16)
        attended = att[b]

        def term(t):
            return jnp.dot(wo[t], attended, preferred_element_type=jnp.float32)

        sums[0, b] = term(opposite).astype(jnp.bfloat16)
        push(sums.at[0, b, low], relay_in.at[0, b], relay_sem.at[0, b], right).start()
        push(sums.at[0, b, high], relay_in.at[1, b], relay_sem.at[1, b], left_x).start()
        to_right = term(right)
        sums[1, b, high] = to_right[400:].astype(jnp.bfloat16)
        push(
            sums.at[1, b, high], final_in.at[0, b, high], final_sem.at[0, b, 0], right
        ).start()
        hold[0, b] = to_right[:400]
        to_left = term(left_x)
        sums[2, b, low] = to_left[:400].astype(jnp.bfloat16)
        push(
            sums.at[2, b, low], final_in.at[1, b, low], final_sem.at[1, b, 0], left_x
        ).start()
        hold[1, b] = to_left[400:]
        own_part[b] = term(tp)
        if b > 0:
            relay(b - 1)
    relay(2)

    row = lax.broadcasted_iota(jnp.int32, (SHARE, SHARE), 0)
    column = lax.broadcasted_iota(jnp.int32, (SHARE, SHARE), 1)
    feature = jnp.where(column < 768, column + column // 24, (column - 768) * 25 + 24)
    unpick = (row == feature).astype(jnp.bfloat16)
    for b in range(3):
        for way, rows in ((0, (low, high)), (1, (high, low))):
            for i in range(2):
                here = final_in.at[way, b, rows[i]]
                push(here, here, final_sem.at[way, b, 1 - i], right).wait_recv()
        total = own_part[b] + final_in[0, b].astype(jnp.float32)
        total += final_in[1, b].astype(jnp.float32)
        total += token_share[:, b * 128 : (b + 1) * 128].astype(jnp.float32)
        rounded = jnp.dot(unpick, total.astype(jnp.bfloat16), preferred_element_type=jnp.float32)
        hidden[:, b * 128 : (b + 1) * 128] = rounded.astype(jnp.bfloat16)
        row_mine[0:1, b * 128 : (b + 1) * 128] = jnp.sum(rounded, axis=0, keepdims=True)
        row_mine[1:2, b * 128 : (b + 1) * 128] = jnp.sum(rounded * rounded, axis=0, keepdims=True)
    row_mine[2:] = jnp.zeros((6, TOK), jnp.float32)
    row_in[pl.ds(tp, 1)] = row_mine[...][None]
    row_copies = [
        to_row(o, row_mine, row_in, row_sem.at[0], row_sem.at[1])
        for o in (opposite, right, left_x)
    ]
    for c in row_copies:
        c.start()

    slot = lax.broadcasted_iota(jnp.int32, (1, 128), 1)
    image = segment(slot, 1)
    owner = jnp.where(image < 3, owners[...], -1)
    cols = jnp.ones((1, 128), jnp.int32)
    start = jnp.zeros((1, 128), jnp.int32)
    for i in range(3):
        cols = jnp.where(image == i, grids[i, 1], cols)
        if i:
            start = jnp.where(image == i, ends[i - 1], start)
    offset = slot - start
    row_half = jnp.zeros((1, 128), jnp.int32)
    for i in range(1, 48):
        row_half += (offset >= i * cols).astype(jnp.int32)
    first_row = 2 * start + offset + row_half * cols
    first_row = 2 * first_row
    owner_square = jnp.broadcast_to(owner, (128, 128))
    owner_down = jnp.transpose(owner_square)
    earlier = lax.broadcasted_iota(jnp.int32, (128, 128), 0) < lax.broadcasted_iota(
        jnp.int32, (128, 128), 1
    )
    rank = jnp.sum(
        jnp.where((owner_down == owner_square) & earlier, 1, 0), axis=0, keepdims=True
    )

    pltpu.make_async_copy(row_in.at[pl.ds(0, 3)], row_in.at[pl.ds(0, 3)], row_sem.at[0]).wait()
    row_total = row_in[0] + row_in[1] + row_in[2] + row_in[3]
    sum_row = row_total[0:1]
    square_row = row_total[1:2]
    gain = jnp.concatenate([p_gain[...], p_gain[...]], axis=0)[None]
    bias = jnp.concatenate([p_bias[...], p_bias[...]], axis=0)[None]

    def send_plane(i, carry):
        base = lax.rem(z + i, SIDE) * 16
        line = lax.broadcasted_iota(jnp.int32, (128, 128), 0)
        found = (owner == base + line // 8) & (rank == (line // 4) % 2)
        first = jnp.sum(jnp.where(found, first_row, 0), axis=1, keepdims=True)
        across = 2 * jnp.sum(jnp.where(found, cols, 0), axis=1, keepdims=True)
        filled = across > 0
        first = jnp.where(filled, first, -10000)
        part = lax.broadcasted_iota(jnp.int32, (128, 1), 0) % 4
        token = lax.broadcasted_iota(jnp.int32, (128, TOK), 1)
        mine = first + part % 2 + (part // 2) * across
        pick = (token == mine).astype(jnp.bfloat16)
        raw = lax.dot_general(
            pick, hidden[...], (((1,), (1,)), ((), ())), preferred_element_type=jnp.float32
        )
        upper, lower = token - first, token - first - across
        any_part = (upper == 0) | (upper == 1) | (lower == 0) | (lower == 1)
        mean = jnp.sum(jnp.where(any_part, sum_row, 0.0), axis=1, keepdims=True) / (4 * D)
        square = jnp.sum(jnp.where(any_part, square_row, 0.0), axis=1, keepdims=True) / (4 * D)
        scale = lax.rsqrt(square - mean * mean + 1e-05)
        value = ((raw - mean) * scale).reshape(16, 8, SHARE) * gain + bias
        value = jnp.where(filled, value.reshape(128, SHARE), 0.0)
        slots[pl.ds(base, 16)] = value.reshape(16, 8, SHARE).astype(jnp.bfloat16)

        def send(j, carry):
            other = base + j

            @pl.when(other != me)
            def _():
                pltpu.make_async_remote_copy(
                    src_ref=slots.at[other],
                    dst_ref=out.at[me],
                    send_sem=send_sem.at[1],
                    recv_sem=out_sem,
                    device_id={"req": other},
                    device_id_type=MESH,
                ).start()

            return carry

        lax.fori_loop(0, 16, send, 0)
        return carry

    lax.fori_loop(0, SIDE, send_plane, 0)
    keep = pltpu.make_async_copy(slots.at[me], out.at[me], own_sem)
    keep.start()
    keep.wait()
    pltpu.make_async_copy(stat_in.at[pl.ds(0, 3)], stat_in.at[pl.ds(0, 3)], stat_sem.at[1]).wait()
    pltpu.make_async_copy(row_in.at[pl.ds(0, 3)], row_in.at[pl.ds(0, 3)], row_sem.at[1]).wait()
    pltpu.make_async_copy(sums, sums, send_sem.at[0]).wait()
    most = out.at[pl.ds(0, 127)]
    pltpu.make_async_copy(most, most, send_sem.at[1]).wait()
    pltpu.make_async_copy(most, most, out_sem).wait()


def finish(x, token_share, left, q_gain, k_gain, grids, owners, p_gain, p_bias, gathered):
    vmem = pl.BlockSpec(memory_space=pltpu.VMEM)
    bf16, f32 = jnp.bfloat16, jnp.float32
    dma = pltpu.SemaphoreType.DMA
    return pl.pallas_call(
        finish_kernel,
        out_shape=jax.ShapeDtypeStruct((128, 8, SHARE), bf16),
        in_specs=[vmem] * 5
        + [pl.BlockSpec(memory_space=pltpu.SMEM)]
        + [vmem] * 3
        + [pl.BlockSpec(memory_space=pl.ANY)],
        out_specs=pl.BlockSpec(memory_space=pl.ANY),
        scratch_shapes=[
            pltpu.VMEM((6, 128, 48, 128), bf16),
            pltpu.VMEM((128, 96, 128), bf16),
            pltpu.VMEM((4, SHARE, 512), bf16),
            pltpu.VMEM((TOK, 1536), f32),
            pltpu.VMEM((4, 128, TOK), bf16),
            pltpu.VMEM((3, 512, 128), bf16),
            pltpu.VMEM((3, SHARE, 128), f32),
            pltpu.VMEM((2, 3, 400, 128), f32),
            pltpu.VMEM((3, 3, SHARE, 128), bf16),
            pltpu.VMEM((2, 3, 400, 128), bf16),
            pltpu.VMEM((2, 3, SHARE, 128), bf16),
            pltpu.VMEM((SHARE, TOK), bf16),
            pltpu.VMEM((8, TOK), f32),
            pltpu.VMEM((4, 8, TOK), f32),
            pltpu.VMEM((8, TOK), f32),
            pltpu.VMEM((4, 8, TOK), f32),
            pltpu.VMEM((128, 8, SHARE), bf16),
            dma((7,)),
            dma((2,)),
            dma((2,)),
            dma((2, 3)),
            dma((2, 3, 2)),
            dma((2,)),
            dma,
            dma,
        ],
        compiler_params=pltpu.CompilerParams(
            collective_id=1, has_side_effects=True, vmem_limit_bytes=60 << 20
        ),
        name="finish",
    )(x, token_share, left, q_gain, k_gain, grids, owners, p_gain, p_bias, gathered)


def body(tokens, norm_gain, w_qkv, q_gain, k_gain, w_out, grids, owners, proj_gain, proj_bias):
    both = jnp.concatenate([w_qkv, w_out.T], axis=1)
    slab = jnp.concatenate(
        [
            both[:24].reshape(24, 16, 128).transpose(1, 0, 2).reshape(384, 128),
            both[24].reshape(16, 128),
        ],
        axis=0,
    )
    gathered = gather_weights(slab)
    normed, token_share = norm_tokens(tokens, norm_gain)
    left = gathered[:, 384:, :].reshape(-1, 2048)
    slot_owner = jnp.pad(owners, (0, 128 - owners.shape[0]), constant_values=-1).reshape(1, 128)
    arrived = finish(
        normed, token_share, left, q_gain.reshape(1, -1), k_gain.reshape(1, -1),
        grids, slot_owner, proj_gain, proj_bias, gathered,
    )
    return arrived.reshape(-1, 4, SHARE)


def solution(mesh):
    placed = (
        P("req", None),
        P(),
        P("req", "tp"),
        P("tp"),
        P("tp"),
        P("tp", "req"),
        P("req", None),
        P("req"),
        P(None, "tp"),
        P(None, "tp"),
    )
    return jax.shard_map(
        body, mesh=mesh, in_specs=placed, out_specs=P("req", None, "tp"), check_vma=False
    )
```

time: 245 us -> 197 us (0.80)
  the two profiles are of different devices: /device:TPU:1 before, /device:TPU:185 now
where the time goes in v2:
time: 197 us; the launch traced here: 196 us
  Pallas kernels  182 us (92%)
  local copies, waits for them, and re-layouts  11.8 us (6%)
  other arithmetic  2.34 us (1%)
    pallas_call x1, Pallas kernels, finish(): pl.pallas_call(finish_kernel, out_shape=jax.ShapeDtypeStruct((128, 8, SHA...  124 us
    pallas_call x1, Pallas kernels, gather_weights(): pl.pallas_call(gather_kernel, out_shape=jax.ShapeDtypeStruct((count, SLAB...  51.3 us
    pallas_call x1, Pallas kernels, norm_tokens(): pl.pallas_call(norm_kernel, out_shape=(jax.ShapeDtypeStruct(tokens.shape,...  7.17 us
    reshape x2, local copies, waits for them, and re-layouts, body(): return arrived.reshape(-1, 4, SHARE)  5.87 us

profile of v2, /device:TPU:185, one launch (start us, length us, event | category | flops | bytes accessed | tf_op | source)
XLA Modules:
  0.0 196.4 jit_solution(4967197350129725281)
XLA Ops:
  0.0 1.2 pad_bitcast_fusion.owners
  1.2 1.3 copy.15.grids
  2.6 0.8 fusion.2
  3.4 1.3 reshape.24.gain
  4.7 0.9 copy_bitcast_fusion.1
  5.6 0.6 pad_maximum_fusion.mine
  6.2 7.2 %norm_tokens.1 = (bf16[384,3200]{1,0:T(8,128)(2,1)}, bf16[800,384]{1,0:T(8,128)(2,1)}) custom-call(bf16[384,3200]{1,0:T(8,128)(2,1)} %tokens.1, f32[1,3200]{1,0:T(1,128)} %reshape.24.gain), custom_call_target="tpu_custom_call" | custom-call | tf_op jit(solution)/shard_map/norm_tokens/pallas_call | solution.py:179
  13.4 51.3 %gather_weights.1.gathered = bf16[128,400,128]{2,1,0:T(8,128)(2,1)} custom-call(bf16[400,128]{1,0:T(8,128)(2,1)} %pad_maximum_fusion.mine), custom_call_target="tpu_custom_call" | custom-call | tf_op jit(solution)/shard_map/gather_weights/pallas_call | solution.py:131
  64.7 1.1 slice.11
  65.8 0.9 copy.21
  66.7 123.8 %finish.1 = bf16[128,8,800]{2,1,0:T(8,128)(2,1)} custom-call(bf16[384,3200]{1,0:T(8,128)(2,1)} %get-tuple-element.7.x_ref, bf16[800,384]{1,0:T(8,128)(2,1)} %get-tuple-element.8.token_share, bf16[128,2048]{1,0:T(8,128)(2,1)} %bitcast.18, f32[1,512]{1,0:T(1,128)} %bitcast.24, f32[1,512]{1,0:T(1,128)} %bitcast.25, s32[3,2]{1,0:T(4,128)} %copy.15.grids, ...), custom_call_target="tpu_custom_call" | custom-call | tf_op jit(solution)/shard_map/finish/pallas_call | solution.py:498
  190.5 3.1 %reshape.31 = bf16[256,4,800]{2,1,0:T(4,128)(2,1)S(1)} reshape(bf16[128,8,800]{2,1,0:T(8,128)(2,1)} %finish.1) | data formatting | bytes 3276800 | tf_op jit(solution)/shard_map/reshape | solution.py:557
  193.7 2.7 %copy.16 = bf16[256,4,800]{0,2,1:T(8,128)(2,1)} copy(bf16[256,4,800]{2,1,0:T(4,128)(2,1)S(1)} %reshape.31) | data formatting | bytes 3276800 | tf_op jit(solution)/shard_map/reshape | solution.py:557

commit v3 on v2

--- a/solution.py
+++ b/solution.py
@@ -24,7 +24,10 @@
     return (z * SIDE + y) * 2 + core
 
 
-def gather_kernel(mine, out, own_sem, send_sem, pair_sem, r1, r2):
+def gather_kernel(
+    w_qkv, w_out, gain, tokens, out, permuted, token_share,
+    mine, held, normed, own_sem, send_sem, pair_sem, token_sem, r1, r2,
+):
     me = lax.axis_index("req")
     z = me // (2 * SIDE)
     y = (me // 2) % SIDE
@@ -46,6 +49,17 @@
     barrier = pltpu.get_barrier_semaphore()
     for other in around + across + [partner]:
         pl.semaphore_signal(barrier, inc=1, device_id={"req": other}, device_id_type=MESH)
+    token_load = pltpu.make_async_copy(tokens, held, token_sem)
+    token_load.start()
+
+    last = jnp.zeros((16, 128), jnp.float32)
+    row = lax.broadcasted_iota(jnp.int32, (16, 128), 0)
+    for b in range(16):
+        weight, at = (w_qkv, 128 * b) if b < 12 else (w_out, 128 * (b - 12))
+        mine[24 * b : 24 * b + 24] = weight[:24, at : at + 128]
+        end = weight[24:25, at : at + 128].astype(jnp.float32)
+        last = jnp.where(row == b, end, last)
+    mine[384:400] = last.astype(jnp.bfloat16)
     pl.semaphore_wait(barrier, 5)
 
     own = pltpu.make_async_copy(mine, out.at[me], own_sem)
@@ -80,6 +94,16 @@
             copy(me, part, None, r1.at[part, way, 0], first[part][way], mine).start()
     for part in range(2):
         spread(part, 0, me, mine)
+    token_load.wait()
+    square = jnp.zeros((TOK, 128), jnp.float32)
+    for j in range(25):
+        x = held[:, 128 * j : 128 * (j + 1)].astype(jnp.float32)
+        square += x * x
+    scale = lax.rsqrt(jnp.sum(square, axis=1, keepdims=True) / D + 1e-06)
+    for j in range(25):
+        x = held[:, 128 * j : 128 * (j + 1)].astype(jnp.float32)
+        normed[:, 128 * j : 128 * (j + 1)] = (x * scale * gain[j : j + 1]).astype(jnp.bfloat16)
+
     for k in range(1, 5):
         for part in range(2):
             p, q = where[part]
@@ -115,9 +139,36 @@
                     for way in range(2):
                         copy(shard, part, way, r2.at[part, way, 3, j], partner).wait_recv()
                     copy(shard, part, None, pair_sem, partner).start()
+            if h < 4:
+                base = 128 * (8 * (h - 1) + j)
+                start = jnp.minimum((base + base // 24) // 128 * 128, D - 384)
+                start = pl.multiple_of(start, 128)
+                source = lax.broadcasted_iota(jnp.int32, (384, 128), 0) + start
+                target = lax.broadcasted_iota(jnp.int32, (384, 128), 1) + base
+                pick = (source == target + target // 24).astype(jnp.bfloat16)
+                permuted[:, pl.ds(pl.multiple_of(base, 128), 128)] = jnp.dot(
+                    normed[:, pl.ds(start, 384)], pick, preferred_element_type=jnp.float32
+                ).astype(jnp.bfloat16)
             return carry
 
         lax.fori_loop(0, SIDE, step, 0)
+        if h == 2:
+            source = lax.broadcasted_iota(jnp.int32, (D, 128), 0)
+            target = lax.broadcasted_iota(jnp.int32, (D, 128), 1)
+            pick = (source == target * 25 + 24).astype(jnp.bfloat16)
+            permuted[:, 3072:] = jnp.dot(
+                normed[...], pick, preferred_element_type=jnp.float32
+            ).astype(jnp.bfloat16)
+        if h == 3:
+            tp = lax.axis_index("tp")
+            window = held[:, pl.ds(pl.multiple_of(tp * 768, 128), 896)]
+            row = lax.broadcasted_iota(jnp.int32, (SHARE, 896), 0)
+            lane = lax.broadcasted_iota(jnp.int32, (SHARE, 896), 1)
+            feature = jnp.where(row < 768, row + row // 24, (row - 768) * 25 + 24)
+            pick = (lane == feature + 32 * tp).astype(jnp.bfloat16)
+            token_share[...] = lax.dot_general(
+                pick, window, (((1,), (1,)), ((), ())), preferred_element_type=jnp.float32
+            ).astype(jnp.bfloat16)
 
     own.wait()
     half_all = out.at[pl.ds(0, 64)]
@@ -126,66 +177,34 @@
     pltpu.make_async_copy(sent, sent, send_sem).wait()
 
 
-def gather_weights(slab):
-    count = lax.axis_size("req")
+def gather_weights(w_qkv, w_out, gain, tokens):
+    vmem, anywhere = pl.BlockSpec(memory_space=pltpu.VMEM), pl.BlockSpec(memory_space=pl.ANY)
+    bf16 = jnp.bfloat16
     return pl.pallas_call(
         gather_kernel,
-        out_shape=jax.ShapeDtypeStruct((count, SLAB, 128), jnp.bfloat16),
-        in_specs=[pl.BlockSpec(memory_space=pl.ANY)],
-        out_specs=pl.BlockSpec(memory_space=pl.ANY),
+        out_shape=(
+            jax.ShapeDtypeStruct((lax.axis_size("req"), SLAB, 128), bf16),
+            jax.ShapeDtypeStruct((TOK, D), bf16),
+            jax.ShapeDtypeStruct((SHARE, TOK), bf16),
+        ),
+        in_specs=[vmem, vmem, vmem, anywhere],
+        out_specs=(anywhere, vmem, vmem),
         scratch_shapes=[
+            pltpu.VMEM((SLAB, 128), bf16),
+            pltpu.VMEM((TOK, D), bf16),
+            pltpu.VMEM((TOK, D), bf16),
+            pltpu.SemaphoreType.DMA,
             pltpu.SemaphoreType.DMA,
             pltpu.SemaphoreType.DMA,
             pltpu.SemaphoreType.DMA,
             pltpu.SemaphoreType.DMA((2, 2, 4)),
             pltpu.SemaphoreType.DMA((2, 2, 4, SIDE)),
         ],
-        compiler_params=pltpu.CompilerParams(collective_id=0, has_side_effects=True),
+        compiler_params=pltpu.CompilerParams(
+            collective_id=0, has_side_effects=True, vmem_limit_bytes=60 << 20
+        ),
         name="gather_weights",
-    )(slab)
-
-
-def norm_kernel(tokens, gain, out, token_share, normed):
-    x = tokens[...].astype(jnp.float32)
-    square = jnp.mean(x * x, axis=1, keepdims=True)
-    normed[...] = (x * lax.rsqrt(square + 1e-06) * gain[...]).astype(jnp.bfloat16)
-    for j in range(24):
-        start = (128 * j + (128 * j) // 24) // 128 * 128
-        width = min(384, D - start)
-        source = lax.broadcasted_iota(jnp.int32, (width, 128), 0) + start
-        target = lax.broadcasted_iota(jnp.int32, (width, 128), 1) + 128 * j
-        pick = (source == target + target // 24).astype(jnp.bfloat16)
-        out[:, 128 * j : 128 * (j + 1)] = jnp.dot(
-            normed[:, start : start + width], pick, preferred_element_type=jnp.float32
-        ).astype(jnp.bfloat16)
-    source = lax.broadcasted_iota(jnp.int32, (D, 128), 0)
-    target = lax.broadcasted_iota(jnp.int32, (D, 128), 1)
-    pick = (source == target * 25 + 24).astype(jnp.bfloat16)
-    out[:, 3072:] = jnp.dot(normed[...], pick, preferred_element_type=jnp.float32).astype(
-        jnp.bfloat16
-    )
-    tp = lax.axis_index("tp")
-    window = tokens[:, pl.ds(pl.multiple_of(tp * 768, 128), 896)]
-    row = lax.broadcasted_iota(jnp.int32, (SHARE, 896), 0)
-    lane = lax.broadcasted_iota(jnp.int32, (SHARE, 896), 1)
-    feature = jnp.where(row < 768, row + row // 24, (row - 768) * 25 + 24)
-    pick = (lane == feature + 32 * tp).astype(jnp.bfloat16)
-    token_share[...] = lax.dot_general(
-        pick, window, (((1,), (1,)), ((), ())), preferred_element_type=jnp.float32
-    ).astype(jnp.bfloat16)
-
-
-def norm_tokens(tokens, gain):
-    return pl.pallas_call(
-        norm_kernel,
-        out_shape=(
-            jax.ShapeDtypeStruct(tokens.shape, jnp.bfloat16),
-            jax.ShapeDtypeStruct((SHARE, tokens.shape[0]), jnp.bfloat16),
-        ),
-        scratch_shapes=[pltpu.VMEM(tokens.shape, jnp.bfloat16)],
-        compiler_params=pltpu.CompilerParams(vmem_limit_bytes=60 << 20),
-        name="norm_tokens",
-    )(tokens, gain.reshape(1, D))
+    )(w_qkv, w_out, gain, tokens)
 
 
 def as_column(row):
@@ -194,9 +213,9 @@
 
 
 def finish_kernel(
-    x_ref, token_share, left, q_gain, k_gain, grids, owners, p_gain, p_bias, gathered,
+    x_ref, token_share, q_gain, k_gain, grids, owners, p_gain, p_bias, gathered,
     out,
-    wq, wo_raw, wo, proj, v_t, att, own_part, hold, sums, relay_in, final_in, hidden,
+    wq, wo_raw, last_raw, last_wide, left, slot_owner, wo, proj, v_t, att, own_part, hold, sums, relay_in, final_in, hidden,
     stat_mine, stat_in, row_mine, row_in, slots,
     load_sem, stat_sem, row_sem, relay_sem, final_sem, send_sem, out_sem, own_sem,
 ):
@@ -224,8 +243,16 @@
         for i in range(6)
     ]
     loads.append(pltpu.make_async_copy(gathered.at[:, pl.ds(288, 96)], wo_raw, load_sem.at[6]))
-    for load in loads:
+    loads.append(
+        pltpu.make_async_copy(gathered.at[:, pl.ds(384, 16)], last_raw, load_sem.at[7])
+    )
+    for load in loads[7:] + loads[:7]:
         load.start()
+
+    loads[7].wait()
+    last_wide[...] = last_raw[...].astype(jnp.float32)
+    for b in range(16):
+        left[:, 128 * b : 128 * (b + 1)] = last_wide[:, b, :].astype(jnp.bfloat16)
 
     def project(i, carry):
         pltpu.make_async_copy(
@@ -291,7 +318,7 @@
     ends = []
     total = 0
     for i in range(3):
-        total = total + grids[i, 0] * grids[i, 1]
+        total = total + grids[0, i] * grids[1, i]
         ends.append(total)
 
     def segment(ids, scale):
@@ -407,11 +434,13 @@
 
     slot = lax.broadcasted_iota(jnp.int32, (1, 128), 1)
     image = segment(slot, 1)
-    owner = jnp.where(image < 3, owners[...], -1)
+    slot_owner[...] = jnp.full((1, 128), -1, jnp.int32)
+    slot_owner[:, : owners.shape[1]] = owners[...]
+    owner = jnp.where(image < 3, slot_owner[...], -1)
     cols = jnp.ones((1, 128), jnp.int32)
     start = jnp.zeros((1, 128), jnp.int32)
     for i in range(3):
-        cols = jnp.where(image == i, grids[i, 1], cols)
+        cols = jnp.where(image == i, grids[1, i], cols)
         if i:
             start = jnp.where(image == i, ends[i - 1], start)
     offset = slot - start
@@ -436,8 +465,11 @@
     gain = jnp.concatenate([p_gain[...], p_gain[...]], axis=0)[None]
     bias = jnp.concatenate([p_bias[...], p_bias[...]], axis=0)[None]
 
-    def send_plane(i, carry):
-        base = lax.rem(z + i, SIDE) * 16
+    def alternate(i):
+        return ((i + 1) // 2) * (1 - 2 * ((i + 1) % 2))
+
+    def fill_plane(i, carry):
+        base = lax.rem(z + alternate(i) + SIDE, SIDE) * 16
         line = lax.broadcasted_iota(jnp.int32, (128, 128), 0)
         found = (owner == base + line // 8) & (rank == (line // 4) % 2)
         first = jnp.sum(jnp.where(found, first_row, 0), axis=1, keepdims=True)
@@ -459,9 +491,16 @@
         value = ((raw - mean) * scale).reshape(16, 8, SHARE) * gain + bias
         value = jnp.where(filled, value.reshape(128, SHARE), 0.0)
         slots[pl.ds(base, 16)] = value.reshape(16, 8, SHARE).astype(jnp.bfloat16)
-
-        def send(j, carry):
-            other = base + j
+        return carry
+
+    y = (me // 2) % SIDE
+    core = me % 2
+
+    def send(i, carry):
+        to_z = lax.rem(z + alternate(4 * (i // 32) + (i % 8 + (i // 8) % 4) % 4) + SIDE, SIDE)
+        to_y = lax.rem(y + alternate(i % 8) + SIDE, SIDE)
+        for flip in range(2):
+            other = shard_of(to_z, to_y, lax.rem(core + flip, 2))
 
             @pl.when(other != me)
             def _():
@@ -474,12 +513,11 @@
                     device_id_type=MESH,
                 ).start()
 
-            return carry
-
-        lax.fori_loop(0, 16, send, 0)
         return carry
 
-    lax.fori_loop(0, SIDE, send_plane, 0)
+    for half in range(2):
+        lax.fori_loop(4 * half, 4 * half + 4, fill_plane, 0)
+        lax.fori_loop(32 * half, 32 * half + 32, send, 0)
     keep = pltpu.make_async_copy(slots.at[me], out.at[me], own_sem)
     keep.start()
     keep.wait()
@@ -491,14 +529,14 @@
     pltpu.make_async_copy(most, most, out_sem).wait()
 
 
-def finish(x, token_share, left, q_gain, k_gain, grids, owners, p_gain, p_bias, gathered):
+def finish(x, token_share, q_gain, k_gain, grids, owners, p_gain, p_bias, gathered):
     vmem = pl.BlockSpec(memory_space=pltpu.VMEM)
     bf16, f32 = jnp.bfloat16, jnp.float32
     dma = pltpu.SemaphoreType.DMA
     return pl.pallas_call(
         finish_kernel,
         out_shape=jax.ShapeDtypeStruct((128, 8, SHARE), bf16),
-        in_specs=[vmem] * 5
+        in_specs=[vmem] * 4
         + [pl.BlockSpec(memory_space=pltpu.SMEM)]
         + [vmem] * 3
         + [pl.BlockSpec(memory_space=pl.ANY)],
@@ -506,6 +544,10 @@
         scratch_shapes=[
             pltpu.VMEM((6, 128, 48, 128), bf16),
             pltpu.VMEM((128, 96, 128), bf16),
+            pltpu.VMEM((128, 16, 128), bf16),
+            pltpu.VMEM((128, 16, 128), f32),
+            pltpu.VMEM((128, 2048), bf16),
+            pltpu.VMEM((1, 128), jnp.int32),
             pltpu.VMEM((4, SHARE, 512), bf16),
             pltpu.VMEM((TOK, 1536), f32),
             pltpu.VMEM((4, 128, TOK), bf16),
@@ -521,7 +563,7 @@
             pltpu.VMEM((8, TOK), f32),
             pltpu.VMEM((4, 8, TOK), f32),
             pltpu.VMEM((128, 8, SHARE), bf16),
-            dma((7,)),
+            dma((8,)),
             dma((2,)),
             dma((2,)),
             dma((2, 3)),
@@ -534,25 +576,16 @@
             collective_id=1, has_side_effects=True, vmem_limit_bytes=60 << 20
         ),
         name="finish",
-    )(x, token_share, left, q_gain, k_gain, grids, owners, p_gain, p_bias, gathered)
+    )(x, token_share, q_gain, k_gain, grids, owners, p_gain, p_bias, gathered)
 
 
 def body(tokens, norm_gain, w_qkv, q_gain, k_gain, w_out, grids, owners, proj_gain, proj_bias):
-    both = jnp.concatenate([w_qkv, w_out.T], axis=1)
-    slab = jnp.concatenate(
-        [
-            both[:24].reshape(24, 16, 128).transpose(1, 0, 2).reshape(384, 128),
-            both[24].reshape(16, 128),
-        ],
-        axis=0,
+    gathered, normed, token_share = gather_weights(
+        w_qkv, w_out.T, norm_gain.reshape(-1, 128), tokens
     )
-    gathered = gather_weights(slab)
-    normed, token_share = norm_tokens(tokens, norm_gain)
-    left = gathered[:, 384:, :].reshape(-1, 2048)
-    slot_owner = jnp.pad(owners, (0, 128 - owners.shape[0]), constant_values=-1).reshape(1, 128)
     arrived = finish(
-        normed, token_share, left, q_gain.reshape(1, -1), k_gain.reshape(1, -1),
-        grids, slot_owner, proj_gain, proj_bias, gathered,
+        normed, token_share, q_gain.reshape(1, -1), k_gain.reshape(1, -1),
+        grids.T, owners.reshape(1, -1), proj_gain, proj_bias, gathered,
     )
     return arrived.reshape(-1, 4, SHARE)
 

time: 197 us -> 182 us (0.924)
  the two profiles are of different devices: /device:TPU:185 before, /device:TPU:1 now
where the time goes in v3:
time: 182 us; the launch traced here: 181 us
  Pallas kernels  175 us (96%)
  local copies, waits for them, and re-layouts  5.87 us (3%)
    pallas_call x1, Pallas kernels, finish(): pl.pallas_call(finish_kernel, out_shape=jax.ShapeDtypeStruct((128, 8, SHA...  115 us
    pallas_call x1, Pallas kernels, gather_weights(): pl.pallas_call(gather_kernel, out_shape=(jax.ShapeDtypeStruct((lax.axis_s...  59.8 us
    reshape x2, local copies, waits for them, and re-layouts, body(): return arrived.reshape(-1, 4, SHARE)  5.87 us

profile of v3, /device:TPU:1, one launch (start us, length us, event | category | flops | bytes accessed | tf_op | source)
XLA Modules:
  0.0 180.8 jit_solution(6810299708620245241)
XLA Ops:
  0.0 59.8 %gather_weights.1 = (bf16[128,400,128]{2,1,0:T(8,128)(2,1)}, bf16[384,3200]{1,0:T(8,128)(2,1)}, bf16[800,384]{1,0:T(8,128)(2,1)}) custom-call(bf16[25,1536]{1,0:T(8,128)(2,1)} %w_qkv.1, bf16[25,512]{1,0:T(8,128)(2,1)} %bitcast.6, f32[25,128]{1,0:T(8,128)} %bitcast.7, bf16[384,3200]{1,0:T(8,128)(2,1)} %tokens.1), custom_call_target="tpu_custom_call" | custom-call | tf_op jit(solution)/shard_map/gather_weights/pallas_call | solution.py:183
  59.8 115.2 %finish.1 = bf16[128,8,800]{2,1,0:T(8,128)(2,1)} custom-call(bf16[384,3200]{1,0:T(8,128)(2,1)} %get-tuple-element.8.x_ref, bf16[800,384]{1,0:T(8,128)(2,1)} %get-tuple-element.9.token_share, f32[1,512]{1,0:T(1,128)} %bitcast.8, f32[1,512]{1,0:T(1,128)} %bitcast.9, s32[2,3]{1,0:T(2,128)} %bitcast.10, s32[1,96]{1,0:T(1,128)} %bitcast.11, f32[4,800]{1,0:T(4,128)} %p_gain.1, ...), custom_call_target="tpu_custom_call" | custom-call | tf_op jit(solution)/shard_map/finish/pallas_call | solution.py:536
  175.0 3.1 %reshape.19 = bf16[256,4,800]{2,1,0:T(4,128)(2,1)S(1)} reshape(bf16[128,8,800]{2,1,0:T(8,128)(2,1)} %finish.1) | data formatting | bytes 3276800 | tf_op jit(solution)/shard_map/reshape | solution.py:590
  178.1 2.7 %copy.12 = bf16[256,4,800]{0,2,1:T(8,128)(2,1)} copy(bf16[256,4,800]{2,1,0:T(4,128)(2,1)S(1)} %reshape.19) | data formatting | bytes 3276800 | tf_op jit(solution)/shard_map/reshape | solution.py:590

commit v4 on v3

--- a/solution.py
+++ b/solution.py
@@ -469,7 +469,7 @@
         return ((i + 1) // 2) * (1 - 2 * ((i + 1) % 2))
 
     def fill_plane(i, carry):
-        base = lax.rem(z + alternate(i) + SIDE, SIDE) * 16
+        base = 16 * i
         line = lax.broadcasted_iota(jnp.int32, (128, 128), 0)
         found = (owner == base + line // 8) & (rank == (line // 4) % 2)
         first = jnp.sum(jnp.where(found, first_row, 0), axis=1, keepdims=True)
@@ -490,15 +490,15 @@
         scale = lax.rsqrt(square - mean * mean + 1e-05)
         value = ((raw - mean) * scale).reshape(16, 8, SHARE) * gain + bias
         value = jnp.where(filled, value.reshape(128, SHARE), 0.0)
-        slots[pl.ds(base, 16)] = value.reshape(16, 8, SHARE).astype(jnp.bfloat16)
+        slots[pl.ds(base, 16)] = value.reshape(16, 2, 4, SHARE).astype(jnp.bfloat16)
         return carry
 
     y = (me // 2) % SIDE
     core = me % 2
 
     def send(i, carry):
-        to_z = lax.rem(z + alternate(4 * (i // 32) + (i % 8 + (i // 8) % 4) % 4) + SIDE, SIDE)
-        to_y = lax.rem(y + alternate(i % 8) + SIDE, SIDE)
+        to_z = lax.rem(z + alternate((15 - i % 8 - i // 8) % 8) + SIDE, SIDE)
+        to_y = lax.rem(y + alternate(7 - i % 8) + SIDE, SIDE)
         for flip in range(2):
             other = shard_of(to_z, to_y, lax.rem(core + flip, 2))
 
@@ -515,9 +515,8 @@
 
         return carry
 
-    for half in range(2):
-        lax.fori_loop(4 * half, 4 * half + 4, fill_plane, 0)
-        lax.fori_loop(32 * half, 32 * half + 32, send, 0)
+    lax.fori_loop(0, SIDE, fill_plane, 0)
+    lax.fori_loop(0, SIDE * SIDE, send, 0)
     keep = pltpu.make_async_copy(slots.at[me], out.at[me], own_sem)
     keep.start()
     keep.wait()
@@ -535,7 +534,7 @@
     dma = pltpu.SemaphoreType.DMA
     return pl.pallas_call(
         finish_kernel,
-        out_shape=jax.ShapeDtypeStruct((128, 8, SHARE), bf16),
+        out_shape=jax.ShapeDtypeStruct((128, 2, 4, SHARE), bf16),
         in_specs=[vmem] * 4
         + [pl.BlockSpec(memory_space=pltpu.SMEM)]
         + [vmem] * 3
@@ -562,7 +561,7 @@
             pltpu.VMEM((4, 8, TOK), f32),
             pltpu.VMEM((8, TOK), f32),
             pltpu.VMEM((4, 8, TOK), f32),
-            pltpu.VMEM((128, 8, SHARE), bf16),
+            pltpu.VMEM((128, 2, 4, SHARE), bf16),
             dma((8,)),
             dma((2,)),
             dma((2,)),

time: 182 us -> 156 us (0.86)
  Pallas kernels: 175 us -> 152 us
  local copies, waits for them, and re-layouts: 5.87 us -> 4.02 us
    pallas_call x1, Pallas kernels: 115 us -> 92.3 us  [finish(): pl.pallas_call(finish_kernel, out_shape=jax.ShapeDtypeStruct((128, 2, 4,...]
    reshape x2 -> x1, local copies, waits for them, and re-layouts: 5.87 us -> 4.02 us  [body(): return arrived.reshape(-1, 4, SHARE)]
where the time goes in v4:
time: 156 us
  Pallas kernels  152 us (97%)
  local copies, waits for them, and re-layouts  4.02 us (3%)
    pallas_call x1, Pallas kernels, finish(): pl.pallas_call(finish_kernel, out_shape=jax.ShapeDtypeStruct((128, 2, 4,...  92.3 us
    pallas_call x1, Pallas kernels, gather_weights(): pl.pallas_call(gather_kernel, out_shape=(jax.ShapeDtypeStruct((lax.axis_s...  59.8 us
    reshape x1, local copies, waits for them, and re-layouts, body(): return arrived.reshape(-1, 4, SHARE)  4.02 us

profile of v4, /device:TPU:1, one launch (start us, length us, event | category | flops | bytes accessed | tf_op | source)
XLA Modules:
  0.0 156.1 jit_solution(13179279568469023019)
XLA Ops:
  0.0 59.8 %gather_weights.1 = (bf16[128,400,128]{2,1,0:T(8,128)(2,1)}, bf16[384,3200]{1,0:T(8,128)(2,1)}, bf16[800,384]{1,0:T(8,128)(2,1)}) custom-call(bf16[25,1536]{1,0:T(8,128)(2,1)} %w_qkv.1, bf16[25,512]{1,0:T(8,128)(2,1)} %bitcast.8, f32[25,128]{1,0:T(8,128)} %bitcast.9, bf16[384,3200]{1,0:T(8,128)(2,1)} %tokens.1), custom_call_target="tpu_custom_call" | custom-call | tf_op jit(solution)/shard_map/gather_weights/pallas_call | solution.py:183
  59.8 92.3 %finish.1 = bf16[128,2,4,800]{3,2,1,0:T(4,128)(2,1)} custom-call(bf16[384,3200]{1,0:T(8,128)(2,1)} %get-tuple-element.8.x_ref, bf16[800,384]{1,0:T(8,128)(2,1)} %get-tuple-element.9.token_share, f32[1,512]{1,0:T(1,128)} %bitcast.10, f32[1,512]{1,0:T(1,128)} %bitcast.11, s32[2,3]{1,0:T(2,128)} %bitcast.12, s32[1,96]{1,0:T(1,128)} %bitcast.13, ...), custom_call_target="tpu_custom_call" | custom-call | tf_op jit(solution)/shard_map/finish/pallas_call | solution.py:535
  152.1 4.0 %copy.11 = bf16[256,4,800]{0,2,1:T(8,128)(2,1)} copy(bf16[256,4,800]{2,1,0:T(4,128)(2,1)} %bitcast.7) | data formatting | bytes 3276800 | tf_op jit(solution)/shard_map/reshape | solution.py:589

commit v5 on v4

--- a/solution.py
+++ b/solution.py
@@ -14,6 +14,7 @@
 MESH = pl.DeviceIdType.MESH
 SIDE = 8
 SLAB = 400
+BLOCKS = (0, 1, 3, 4, 6, 7, 9, 10, 2, 5, 8, 11)
 PART = ((0, 200), (200, 200))
 HALF = 104
 TOK = 384
@@ -55,7 +56,7 @@
     last = jnp.zeros((16, 128), jnp.float32)
     row = lax.broadcasted_iota(jnp.int32, (16, 128), 0)
     for b in range(16):
-        weight, at = (w_qkv, 128 * b) if b < 12 else (w_out, 128 * (b - 12))
+        weight, at = (w_qkv, 128 * BLOCKS[b]) if b < 12 else (w_out, 128 * (b - 12))
         mine[24 * b : 24 * b + 24] = weight[:24, at : at + 128]
         end = weight[24:25, at : at + 128].astype(jnp.float32)
         last = jnp.where(row == b, end, last)
@@ -94,16 +95,6 @@
             copy(me, part, None, r1.at[part, way, 0], first[part][way], mine).start()
     for part in range(2):
         spread(part, 0, me, mine)
-    token_load.wait()
-    square = jnp.zeros((TOK, 128), jnp.float32)
-    for j in range(25):
-        x = held[:, 128 * j : 128 * (j + 1)].astype(jnp.float32)
-        square += x * x
-    scale = lax.rsqrt(jnp.sum(square, axis=1, keepdims=True) / D + 1e-06)
-    for j in range(25):
-        x = held[:, 128 * j : 128 * (j + 1)].astype(jnp.float32)
-        normed[:, 128 * j : 128 * (j + 1)] = (x * scale * gain[j : j + 1]).astype(jnp.bfloat16)
-
     for k in range(1, 5):
         for part in range(2):
             p, q = where[part]
@@ -119,6 +110,16 @@
                 for way in range(2):
                     copy(shard, part, way, r1.at[part, way, 3], partner).wait_recv()
                 spread(part, 7, shard)
+    token_load.wait()
+    square = jnp.zeros((TOK, 128), jnp.float32)
+    for j in range(25):
+        x = held[:, 128 * j : 128 * (j + 1)].astype(jnp.float32)
+        square += x * x
+    scale = lax.rsqrt(jnp.sum(square, axis=1, keepdims=True) / D + 1e-06)
+    for j in range(25):
+        x = held[:, 128 * j : 128 * (j + 1)].astype(jnp.float32)
+        normed[:, 128 * j : 128 * (j + 1)] = (x * scale * gain[j : j + 1]).astype(jnp.bfloat16)
+
     for h in range(1, 5):
 
         def step(j, carry):
@@ -216,7 +217,7 @@
     x_ref, token_share, q_gain, k_gain, grids, owners, p_gain, p_bias, gathered,
     out,
     wq, wo_raw, last_raw, last_wide, left, slot_owner, wo, proj, v_t, att, own_part, hold, sums, relay_in, final_in, hidden,
-    stat_mine, stat_in, row_mine, row_in, slots,
+    stat_mine, stat_in, row_mine, row_in, picks, members, raws, slots,
     load_sem, stat_sem, row_sem, relay_sem, final_sem, send_sem, out_sem, own_sem,
 ):
     me = lax.axis_index("req")
@@ -269,7 +270,7 @@
         proj[:, pl.ds(at, 256)] = total
         return carry
 
-    lax.fori_loop(0, 6, project, 0)
+    lax.fori_loop(0, 4, project, 0)
 
     pl.semaphore_wait(barrier, devices - 1 + 3)
 
@@ -286,8 +287,8 @@
     q_sum = jnp.zeros((TOK, 1), jnp.float32)
     k_sum = jnp.zeros((TOK, 1), jnp.float32)
     for h in range(4):
-        q = proj[:, h * 384 : h * 384 + 128]
-        k = proj[:, h * 384 + 128 : h * 384 + 256]
+        q = proj[:, h * 256 : h * 256 + 128]
+        k = proj[:, h * 256 + 128 : h * 256 + 256]
         q_sum += jnp.sum(q * q, axis=1, keepdims=True)
         k_sum += jnp.sum(k * k, axis=1, keepdims=True)
     lane = lax.broadcasted_iota(jnp.int32, (TOK, 128), 1)
@@ -301,8 +302,9 @@
     for c in stat_copies:
         c.start()
 
+    lax.fori_loop(4, 6, project, 0)
     for h in range(4):
-        v_t[h] = jnp.transpose(proj[:, h * 384 + 256 : h * 384 + 384]).astype(jnp.bfloat16)
+        v_t[h] = jnp.transpose(proj[:, 1024 + h * 128 : 1152 + h * 128]).astype(jnp.bfloat16)
     loads[6].wait()
 
     def pack(t, carry):
@@ -335,7 +337,7 @@
     q_scale = as_column(scales[0:1])
     k_scale = as_column(scales[1:2])
     for h in range(4):
-        at = h * 384
+        at = h * 256
         head = slice(h * 128, (h + 1) * 128)
         proj[:, at : at + 128] = proj[:, at : at + 128] * q_scale * q_gain[:, head]
         proj[:, at + 128 : at + 256] = proj[:, at + 128 : at + 256] * k_scale * k_gain[:, head]
@@ -368,7 +370,7 @@
             lax.broadcasted_iota(jnp.int32, (TOK, 128), 1) + 128 * b, 4
         )
         for h in range(4):
-            at = h * 384
+            at = h * 256
             scores = lax.dot_general(
                 proj[:, at + 128 : at + 256],
                 proj[q_at, at : at + 128],
@@ -406,31 +408,6 @@
         if b > 0:
             relay(b - 1)
     relay(2)
-
-    row = lax.broadcasted_iota(jnp.int32, (SHARE, SHARE), 0)
-    column = lax.broadcasted_iota(jnp.int32, (SHARE, SHARE), 1)
-    feature = jnp.where(column < 768, column + column // 24, (column - 768) * 25 + 24)
-    unpick = (row == feature).astype(jnp.bfloat16)
-    for b in range(3):
-        for way, rows in ((0, (low, high)), (1, (high, low))):
-            for i in range(2):
-                here = final_in.at[way, b, rows[i]]
-                push(here, here, final_sem.at[way, b, 1 - i], right).wait_recv()
-        total = own_part[b] + final_in[0, b].astype(jnp.float32)
-        total += final_in[1, b].astype(jnp.float32)
-        total += token_share[:, b * 128 : (b + 1) * 128].astype(jnp.float32)
-        rounded = jnp.dot(unpick, total.astype(jnp.bfloat16), preferred_element_type=jnp.float32)
-        hidden[:, b * 128 : (b + 1) * 128] = rounded.astype(jnp.bfloat16)
-        row_mine[0:1, b * 128 : (b + 1) * 128] = jnp.sum(rounded, axis=0, keepdims=True)
-        row_mine[1:2, b * 128 : (b + 1) * 128] = jnp.sum(rounded * rounded, axis=0, keepdims=True)
-    row_mine[2:] = jnp.zeros((6, TOK), jnp.float32)
-    row_in[pl.ds(tp, 1)] = row_mine[...][None]
-    row_copies = [
-        to_row(o, row_mine, row_in, row_sem.at[0], row_sem.at[1])
-        for o in (opposite, right, left_x)
-    ]
-    for c in row_copies:
-        c.start()
 
     slot = lax.broadcasted_iota(jnp.int32, (1, 128), 1)
     image = segment(slot, 1)
@@ -458,17 +435,7 @@
         jnp.where((owner_down == owner_square) & earlier, 1, 0), axis=0, keepdims=True
     )
 
-    pltpu.make_async_copy(row_in.at[pl.ds(0, 3)], row_in.at[pl.ds(0, 3)], row_sem.at[0]).wait()
-    row_total = row_in[0] + row_in[1] + row_in[2] + row_in[3]
-    sum_row = row_total[0:1]
-    square_row = row_total[1:2]
-    gain = jnp.concatenate([p_gain[...], p_gain[...]], axis=0)[None]
-    bias = jnp.concatenate([p_bias[...], p_bias[...]], axis=0)[None]
-
-    def alternate(i):
-        return ((i + 1) // 2) * (1 - 2 * ((i + 1) % 2))
-
-    def fill_plane(i, carry):
+    def table(i, carry):
         base = 16 * i
         line = lax.broadcasted_iota(jnp.int32, (128, 128), 0)
         found = (owner == base + line // 8) & (rank == (line // 4) % 2)
@@ -479,18 +446,66 @@
         part = lax.broadcasted_iota(jnp.int32, (128, 1), 0) % 4
         token = lax.broadcasted_iota(jnp.int32, (128, TOK), 1)
         mine = first + part % 2 + (part // 2) * across
-        pick = (token == mine).astype(jnp.bfloat16)
-        raw = lax.dot_general(
-            pick, hidden[...], (((1,), (1,)), ((), ())), preferred_element_type=jnp.float32
-        )
+        picks[i] = (token == mine).astype(jnp.bfloat16)
         upper, lower = token - first, token - first - across
         any_part = (upper == 0) | (upper == 1) | (lower == 0) | (lower == 1)
-        mean = jnp.sum(jnp.where(any_part, sum_row, 0.0), axis=1, keepdims=True) / (4 * D)
-        square = jnp.sum(jnp.where(any_part, square_row, 0.0), axis=1, keepdims=True) / (4 * D)
+        members[i] = any_part.astype(jnp.float32)
+        return carry
+
+    lax.fori_loop(0, SIDE, table, 0)
+
+    row = lax.broadcasted_iota(jnp.int32, (SHARE, SHARE), 0)
+    column = lax.broadcasted_iota(jnp.int32, (SHARE, SHARE), 1)
+    feature = jnp.where(column < 768, column + column // 24, (column - 768) * 25 + 24)
+    unpick = (row == feature).astype(jnp.bfloat16)
+    for b in range(3):
+        for way, rows in ((0, (low, high)), (1, (high, low))):
+            for i in range(2):
+                here = final_in.at[way, b, rows[i]]
+                push(here, here, final_sem.at[way, b, 1 - i], right).wait_recv()
+        total = own_part[b] + final_in[0, b].astype(jnp.float32)
+        total += final_in[1, b].astype(jnp.float32)
+        total += token_share[:, b * 128 : (b + 1) * 128].astype(jnp.float32)
+        rounded = jnp.dot(unpick, total.astype(jnp.bfloat16), preferred_element_type=jnp.float32)
+        hidden[:, b * 128 : (b + 1) * 128] = rounded.astype(jnp.bfloat16)
+        row_mine[0:1, b * 128 : (b + 1) * 128] = jnp.sum(rounded, axis=0, keepdims=True)
+        row_mine[1:2, b * 128 : (b + 1) * 128] = jnp.sum(rounded * rounded, axis=0, keepdims=True)
+    row_mine[2:] = jnp.zeros((6, TOK), jnp.float32)
+    row_in[pl.ds(tp, 1)] = row_mine[...][None]
+    row_copies = [
+        to_row(o, row_mine, row_in, row_sem.at[0], row_sem.at[1])
+        for o in (opposite, right, left_x)
+    ]
+    for c in row_copies:
+        c.start()
+
+    def gather_rows(i, carry):
+        raws[i] = lax.dot_general(
+            picks[i], hidden[...], (((1,), (1,)), ((), ())), preferred_element_type=jnp.float32
+        )
+        return carry
+
+    lax.fori_loop(0, SIDE, gather_rows, 0)
+
+    pltpu.make_async_copy(row_in.at[pl.ds(0, 3)], row_in.at[pl.ds(0, 3)], row_sem.at[0]).wait()
+    row_total = row_in[0] + row_in[1] + row_in[2] + row_in[3]
+    sum_row = row_total[0:1]
+    square_row = row_total[1:2]
+    gain = jnp.concatenate([p_gain[...], p_gain[...]], axis=0)[None]
+    bias = jnp.concatenate([p_bias[...], p_bias[...]], axis=0)[None]
+
+    def alternate(i):
+        return ((i + 1) // 2) * (1 - 2 * ((i + 1) % 2))
+
+    def fill_plane(i, carry):
+        member = members[i]
+        mean = jnp.sum(member * sum_row, axis=1, keepdims=True) / (4 * D)
+        square = jnp.sum(member * square_row, axis=1, keepdims=True) / (4 * D)
+        filled = jnp.sum(member, axis=1, keepdims=True) > 0.5
         scale = lax.rsqrt(square - mean * mean + 1e-05)
-        value = ((raw - mean) * scale).reshape(16, 8, SHARE) * gain + bias
+        value = ((raws[i] - mean) * scale).reshape(16, 8, SHARE) * gain + bias
         value = jnp.where(filled, value.reshape(128, SHARE), 0.0)
-        slots[pl.ds(base, 16)] = value.reshape(16, 2, 4, SHARE).astype(jnp.bfloat16)
+        slots[pl.ds(16 * i, 16)] = value.reshape(16, 2, 4, SHARE).astype(jnp.bfloat16)
         return carry
 
     y = (me // 2) % SIDE
@@ -561,6 +576,9 @@
             pltpu.VMEM((4, 8, TOK), f32),
             pltpu.VMEM((8, TOK), f32),
             pltpu.VMEM((4, 8, TOK), f32),
+            pltpu.VMEM((SIDE, 128, TOK), bf16),
+            pltpu.VMEM((SIDE, 128, TOK), f32),
+            pltpu.VMEM((SIDE, 128, SHARE), f32),
             pltpu.VMEM((128, 2, 4, SHARE), bf16),
             dma((8,)),
             dma((2,)),

time: 156 us -> 154 us (0.987)
  Pallas kernels: 152 us -> 150 us
    pallas_call x1, Pallas kernels: 92.3 us -> 89.6 us  [finish(): pl.pallas_call(finish_kernel, out_shape=jax.ShapeDtypeStruct((128, 2, 4,...]
where the time goes in v5:
time: 154 us
  Pallas kernels  150 us (97%)
  local copies, waits for them, and re-layouts  4.02 us (3%)
    pallas_call x1, Pallas kernels, finish(): pl.pallas_call(finish_kernel, out_shape=jax.ShapeDtypeStruct((128, 2, 4,...  89.6 us
    pallas_call x1, Pallas kernels, gather_weights(): pl.pallas_call(gather_kernel, out_shape=(jax.ShapeDtypeStruct((lax.axis_s...  60.2 us
    reshape x1, local copies, waits for them, and re-layouts, body(): return arrived.reshape(-1, 4, SHARE)  4.02 us

profile of v5, /device:TPU:1, one launch (start us, length us, event | category | flops | bytes accessed | tf_op | source)
XLA Modules:
  0.0 153.9 jit_solution(7463102106672910370)
XLA Ops:
  0.0 60.2 %gather_weights.1 = (bf16[128,400,128]{2,1,0:T(8,128)(2,1)}, bf16[384,3200]{1,0:T(8,128)(2,1)}, bf16[800,384]{1,0:T(8,128)(2,1)}) custom-call(bf16[25,1536]{1,0:T(8,128)(2,1)} %w_qkv.1, bf16[25,512]{1,0:T(8,128)(2,1)} %bitcast.8, f32[25,128]{1,0:T(8,128)} %bitcast.9, bf16[384,3200]{1,0:T(8,128)(2,1)} %tokens.1), custom_call_target="tpu_custom_call" | custom-call | tf_op jit(solution)/shard_map/gather_weights/pallas_call | solution.py:184
  60.2 89.6 %finish.1 = bf16[128,2,4,800]{3,2,1,0:T(4,128)(2,1)} custom-call(bf16[384,3200]{1,0:T(8,128)(2,1)} %get-tuple-element.8.x_ref, bf16[800,384]{1,0:T(8,128)(2,1)} %get-tuple-element.9.token_share, f32[1,512]{1,0:T(1,128)} %bitcast.10, f32[1,512]{1,0:T(1,128)} %bitcast.11, s32[2,3]{1,0:T(2,128)} %bitcast.12, s32[1,96]{1,0:T(1,128)} %bitcast.13, ...), custom_call_target="tpu_custom_call" | custom-call | tf_op jit(solution)/shard_map/finish/pallas_call | solution.py:550
  149.9 4.0 %copy.11 = bf16[256,4,800]{0,2,1:T(8,128)(2,1)} copy(bf16[256,4,800]{2,1,0:T(4,128)(2,1)} %bitcast.7) | data formatting | bytes 3276800 | tf_op jit(solution)/shard_map/reshape | solution.py:607

commit v6 on v5

--- a/solution.py
+++ b/solution.py
@@ -26,8 +26,9 @@
 
 
 def gather_kernel(
-    w_qkv, w_out, gain, tokens, out, permuted, token_share,
-    mine, held, normed, own_sem, send_sem, pair_sem, token_sem, r1, r2,
+    w_qkv, w_out, gain, tokens, out, permuted_out, share_out,
+    mine, held, normed, permuted, token_share,
+    own_sem, send_sem, pair_sem, token_sem, write_sem, r1, r2,
 ):
     me = lax.axis_index("req")
     z = me // (2 * SIDE)
@@ -170,8 +171,16 @@
             token_share[...] = lax.dot_general(
                 pick, window, (((1,), (1,)), ((), ())), preferred_element_type=jnp.float32
             ).astype(jnp.bfloat16)
+            writes = [
+                pltpu.make_async_copy(permuted, permuted_out, write_sem.at[0]),
+                pltpu.make_async_copy(token_share, share_out, write_sem.at[1]),
+            ]
+            for write in writes:
+                write.start()
 
     own.wait()
+    for write in writes:
+        write.wait()
     half_all = out.at[pl.ds(0, 64)]
     pltpu.make_async_copy(half_all, half_all, pair_sem).wait()
     sent = out.at[pl.ds(0, 127)]
@@ -189,15 +198,18 @@
             jax.ShapeDtypeStruct((SHARE, TOK), bf16),
         ),
         in_specs=[vmem, vmem, vmem, anywhere],
-        out_specs=(anywhere, vmem, vmem),
+        out_specs=(anywhere, anywhere, anywhere),
         scratch_shapes=[
             pltpu.VMEM((SLAB, 128), bf16),
             pltpu.VMEM((TOK, D), bf16),
             pltpu.VMEM((TOK, D), bf16),
+            pltpu.VMEM((TOK, D), bf16),
+            pltpu.VMEM((SHARE, TOK), bf16),
             pltpu.SemaphoreType.DMA,
             pltpu.SemaphoreType.DMA,
             pltpu.SemaphoreType.DMA,
             pltpu.SemaphoreType.DMA,
+            pltpu.SemaphoreType.DMA((2,)),
             pltpu.SemaphoreType.DMA((2, 2, 4)),
             pltpu.SemaphoreType.DMA((2, 2, 4, SIDE)),
         ],
@@ -214,9 +226,9 @@
 
 
 def finish_kernel(
-    x_ref, token_share, q_gain, k_gain, grids, owners, p_gain, p_bias, gathered,
+    x_hbm, share_hbm, q_gain, k_gain, grids, owners, p_gain, p_bias, gathered,
     out,
-    wq, wo_raw, last_raw, last_wide, left, slot_owner, wo, proj, v_t, att, own_part, hold, sums, relay_in, final_in, hidden,
+    x_ref, token_share, wq, wo_raw, last_raw, last_wide, left, slot_owner, wo, proj, v_t, att, own_part, hold, sums, relay_in, final_in, hidden,
     stat_mine, stat_in, row_mine, row_in, picks, members, raws, slots,
     load_sem, stat_sem, row_sem, relay_sem, final_sem, send_sem, out_sem, own_sem,
 ):
@@ -228,6 +240,17 @@
     opposite = lax.rem(tp + 2, 4)
     left_x = lax.rem(tp + 3, 4)
 
+    def load_block(i):
+        at = pl.multiple_of(48 * i, 8)
+        return pltpu.make_async_copy(gathered.at[:, pl.ds(at, 48)], wq.at[i], load_sem.at[i])
+
+    wo_load = pltpu.make_async_copy(gathered.at[:, pl.ds(288, 96)], wo_raw, load_sem.at[6])
+    last_load = pltpu.make_async_copy(gathered.at[:, pl.ds(384, 16)], last_raw, load_sem.at[7])
+    x_load = pltpu.make_async_copy(x_hbm, x_ref, load_sem.at[8])
+    share_load = pltpu.make_async_copy(share_hbm, token_share, load_sem.at[9])
+    for load in (last_load, x_load, load_block(0), load_block(1)):
+        load.start()
+
     barrier = pltpu.get_barrier_semaphore()
 
     def greet(i, carry):
@@ -239,26 +262,18 @@
     for other in (right, opposite, left_x):
         pl.semaphore_signal(barrier, inc=1, device_id={"tp": other}, device_id_type=MESH)
 
-    loads = [
-        pltpu.make_async_copy(gathered.at[:, pl.ds(48 * i, 48)], wq.at[i], load_sem.at[i])
-        for i in range(6)
-    ]
-    loads.append(pltpu.make_async_copy(gathered.at[:, pl.ds(288, 96)], wo_raw, load_sem.at[6]))
-    loads.append(
-        pltpu.make_async_copy(gathered.at[:, pl.ds(384, 16)], last_raw, load_sem.at[7])
-    )
-    for load in loads[7:] + loads[:7]:
-        load.start()
-
-    loads[7].wait()
+    last_load.wait()
     last_wide[...] = last_raw[...].astype(jnp.float32)
     for b in range(16):
         left[:, 128 * b : 128 * (b + 1)] = last_wide[:, b, :].astype(jnp.bfloat16)
 
     def project(i, carry):
-        pltpu.make_async_copy(
-            gathered.at[:, pl.ds(0, 48)], wq.at[i], load_sem.at[i]
-        ).wait()
+        load_block(i).wait()
+
+        @pl.when(i < 4)
+        def _():
+            load_block(i + 2).start()
+
         weight = jnp.concatenate(
             [wq[i, :, :24].reshape(3072, 128), wq[i, :, 24:].reshape(3072, 128)], axis=1
         )
@@ -270,7 +285,10 @@
         proj[:, pl.ds(at, 256)] = total
         return carry
 
+    x_load.wait()
     lax.fori_loop(0, 4, project, 0)
+    wo_load.start()
+    share_load.start()
 
     pl.semaphore_wait(barrier, devices - 1 + 3)
 
@@ -305,7 +323,7 @@
     lax.fori_loop(4, 6, project, 0)
     for h in range(4):
         v_t[h] = jnp.transpose(proj[:, 1024 + h * 128 : 1152 + h * 128]).astype(jnp.bfloat16)
-    loads[6].wait()
+    wo_load.wait()
 
     def pack(t, carry):
         at = pl.multiple_of(t * 32, 32)
@@ -454,6 +472,7 @@
 
     lax.fori_loop(0, SIDE, table, 0)
 
+    share_load.wait()
     row = lax.broadcasted_iota(jnp.int32, (SHARE, SHARE), 0)
     column = lax.broadcasted_iota(jnp.int32, (SHARE, SHARE), 1)
     feature = jnp.where(column < 768, column + column // 24, (column - 768) * 25 + 24)
@@ -550,12 +569,15 @@
     return pl.pallas_call(
         finish_kernel,
         out_shape=jax.ShapeDtypeStruct((128, 2, 4, SHARE), bf16),
-        in_specs=[vmem] * 4
+        in_specs=[pl.BlockSpec(memory_space=pl.ANY)] * 2
+        + [vmem] * 2
         + [pl.BlockSpec(memory_space=pltpu.SMEM)]
         + [vmem] * 3
         + [pl.BlockSpec(memory_space=pl.ANY)],
         out_specs=pl.BlockSpec(memory_space=pl.ANY),
         scratch_shapes=[
+            pltpu.VMEM((TOK, D), bf16),
+            pltpu.VMEM((SHARE, TOK), bf16),
             pltpu.VMEM((6, 128, 48, 128), bf16),
             pltpu.VMEM((128, 96, 128), bf16),
             pltpu.VMEM((128, 16, 128), bf16),
@@ -580,7 +602,7 @@
             pltpu.VMEM((SIDE, 128, TOK), f32),
             pltpu.VMEM((SIDE, 128, SHARE), f32),
             pltpu.VMEM((128, 2, 4, SHARE), bf16),
-            dma((8,)),
+            dma((10,)),
             dma((2,)),
             dma((2,)),
             dma((2, 3)),

time: 154 us -> 150 us (0.974)
  Pallas kernels: 150 us -> 146 us
    pallas_call x1, Pallas kernels: 89.6 us -> 87.3 us  [finish(): pl.pallas_call(finish_kernel, out_shape=jax.ShapeDtypeStruct((128, 2, 4,...]
    pallas_call x1, Pallas kernels: 60.2 us -> 58.6 us  [gather_weights(): pl.pallas_call(gather_kernel, out_shape=(jax.ShapeDtypeStruct((lax.axis_s...]
where the time goes in v6:
time: 150 us
  Pallas kernels  146 us (97%)
  local copies, waits for them, and re-layouts  4.02 us (3%)
    pallas_call x1, Pallas kernels, finish(): pl.pallas_call(finish_kernel, out_shape=jax.ShapeDtypeStruct((128, 2, 4,...  87.3 us
    pallas_call x1, Pallas kernels, gather_weights(): pl.pallas_call(gather_kernel, out_shape=(jax.ShapeDtypeStruct((lax.axis_s...  58.6 us
    reshape x1, local copies, waits for them, and re-layouts, body(): return arrived.reshape(-1, 4, SHARE)  4.02 us

profile of v6, /device:TPU:1, one launch (start us, length us, event | category | flops | bytes accessed | tf_op | source)
XLA Modules:
  0.0 150.0 jit_solution(3880334707063310604)
XLA Ops:
  0.0 58.6 %gather_weights.1 = (bf16[128,400,128]{2,1,0:T(8,128)(2,1)}, bf16[384,3200]{1,0:T(8,128)(2,1)}, bf16[800,384]{1,0:T(8,128)(2,1)}) custom-call(bf16[25,1536]{1,0:T(8,128)(2,1)} %w_qkv.1, bf16[25,512]{1,0:T(8,128)(2,1)} %bitcast.8, f32[25,128]{1,0:T(8,128)} %bitcast.9, bf16[384,3200]{1,0:T(8,128)(2,1)} %tokens.1), custom_call_target="tpu_custom_call" | custom-call | tf_op jit(solution)/shard_map/gather_weights/pallas_call | solution.py:193
  58.6 87.3 %finish.1 = bf16[128,2,4,800]{3,2,1,0:T(4,128)(2,1)} custom-call(bf16[384,3200]{1,0:T(8,128)(2,1)} %get-tuple-element.8.x_hbm, bf16[800,384]{1,0:T(8,128)(2,1)} %get-tuple-element.9.share_hbm, f32[1,512]{1,0:T(1,128)} %bitcast.10, f32[1,512]{1,0:T(1,128)} %bitcast.11, s32[2,3]{1,0:T(2,128)} %bitcast.12, s32[1,96]{1,0:T(1,128)} %bitcast.13, f32[4,800]{1,0:T(4,128)} %p_gain.1, ...), custom_call_target="tpu_custom_call" | custom-call | tf_op jit(solution)/shard_map/finish/pallas_call | solution.py:569
  146.0 4.0 %copy.11 = bf16[256,4,800]{0,2,1:T(8,128)(2,1)} copy(bf16[256,4,800]{2,1,0:T(4,128)(2,1)} %bitcast.7) | data formatting | bytes 3276800 | tf_op jit(solution)/shard_map/reshape | solution.py:629

commit v7 on v6

--- a/solution.py
+++ b/solution.py
@@ -227,9 +227,9 @@
 
 def finish_kernel(
     x_hbm, share_hbm, q_gain, k_gain, grids, owners, p_gain, p_bias, gathered,
-    out,
+    out, out_end,
     x_ref, token_share, wq, wo_raw, last_raw, last_wide, left, slot_owner, wo, proj, v_t, att, own_part, hold, sums, relay_in, final_in, hidden,
-    stat_mine, stat_in, row_mine, row_in, picks, members, raws, slots,
+    stat_mine, stat_in, row_mine, row_in, picks, members, raws, slots, slots_end,
     load_sem, stat_sem, row_sem, relay_sem, final_sem, send_sem, out_sem, own_sem,
 ):
     me = lax.axis_index("req")
@@ -524,7 +524,15 @@
         scale = lax.rsqrt(square - mean * mean + 1e-05)
         value = ((raws[i] - mean) * scale).reshape(16, 8, SHARE) * gain + bias
         value = jnp.where(filled, value.reshape(128, SHARE), 0.0)
-        slots[pl.ds(16 * i, 16)] = value.reshape(16, 2, 4, SHARE).astype(jnp.bfloat16)
+        slots[pl.ds(16 * i, 16)] = value[:, :768].reshape(16, 2, 4, 768).astype(jnp.bfloat16)
+        end = jnp.concatenate([value[:, 768:]] * 4, axis=1)
+        row = lax.broadcasted_iota(jnp.int32, (128, 128), 0)
+        lane = lax.broadcasted_iota(jnp.int32, (128, 128), 1)
+        end = jnp.where(row % 4 == lane // 32, end, 0.0).astype(jnp.bfloat16)
+        four = lax.broadcasted_iota(jnp.int32, (32, 128), 1) // 4
+        four = (four == lax.broadcasted_iota(jnp.int32, (32, 128), 0)).astype(jnp.bfloat16)
+        end = jnp.dot(four, end, preferred_element_type=jnp.float32)
+        slots_end[pl.ds(16 * i, 16)] = end.reshape(16, 2, 128).astype(jnp.bfloat16)
         return carry
 
     y = (me // 2) % SIDE
@@ -538,28 +546,31 @@
 
             @pl.when(other != me)
             def _():
-                pltpu.make_async_remote_copy(
-                    src_ref=slots.at[other],
-                    dst_ref=out.at[me],
-                    send_sem=send_sem.at[1],
-                    recv_sem=out_sem,
-                    device_id={"req": other},
-                    device_id_type=MESH,
-                ).start()
+                for n, (source, into) in enumerate(((slots, out), (slots_end, out_end))):
+                    pltpu.make_async_remote_copy(
+                        src_ref=source.at[other],
+                        dst_ref=into.at[me],
+                        send_sem=send_sem.at[1 + n],
+                        recv_sem=out_sem.at[n],
+                        device_id={"req": other},
+                        device_id_type=MESH,
+                    ).start()
 
         return carry
 
     lax.fori_loop(0, SIDE, fill_plane, 0)
     lax.fori_loop(0, SIDE * SIDE, send, 0)
-    keep = pltpu.make_async_copy(slots.at[me], out.at[me], own_sem)
-    keep.start()
-    keep.wait()
+    for n, (source, into) in enumerate(((slots, out), (slots_end, out_end))):
+        keep = pltpu.make_async_copy(source.at[me], into.at[me], own_sem.at[n])
+        keep.start()
+        keep.wait()
     pltpu.make_async_copy(stat_in.at[pl.ds(0, 3)], stat_in.at[pl.ds(0, 3)], stat_sem.at[1]).wait()
     pltpu.make_async_copy(row_in.at[pl.ds(0, 3)], row_in.at[pl.ds(0, 3)], row_sem.at[1]).wait()
     pltpu.make_async_copy(sums, sums, send_sem.at[0]).wait()
-    most = out.at[pl.ds(0, 127)]
-    pltpu.make_async_copy(most, most, send_sem.at[1]).wait()
-    pltpu.make_async_copy(most, most, out_sem).wait()
+    for n, into in enumerate((out, out_end)):
+        most = into.at[pl.ds(0, 127)]
+        pltpu.make_async_copy(most, most, send_sem.at[1 + n]).wait()
+        pltpu.make_async_copy(most, most, out_sem.at[n]).wait()
 
 
 def finish(x, token_share, q_gain, k_gain, grids, owners, p_gain, p_bias, gathered):
@@ -568,13 +579,16 @@
     dma = pltpu.SemaphoreType.DMA
     return pl.pallas_call(
         finish_kernel,
-        out_shape=jax.ShapeDtypeStruct((128, 2, 4, SHARE), bf16),
+        out_shape=(
+            jax.ShapeDtypeStruct((128, 2, 4, 768), bf16),
+            jax.ShapeDtypeStruct((128, 2, 128), bf16),
+        ),
         in_specs=[pl.BlockSpec(memory_space=pl.ANY)] * 2
         + [vmem] * 2
         + [pl.BlockSpec(memory_space=pltpu.SMEM)]
         + [vmem] * 3
         + [pl.BlockSpec(memory_space=pl.ANY)],
-        out_specs=pl.BlockSpec(memory_space=pl.ANY),
+        out_specs=[pl.BlockSpec(memory_space=pl.ANY)] * 2,
         scratch_shapes=[
             pltpu.VMEM((TOK, D), bf16),
             pltpu.VMEM((SHARE, TOK), bf16),
@@ -601,15 +615,16 @@
             pltpu.VMEM((SIDE, 128, TOK), bf16),
             pltpu.VMEM((SIDE, 128, TOK), f32),
             pltpu.VMEM((SIDE, 128, SHARE), f32),
-            pltpu.VMEM((128, 2, 4, SHARE), bf16),
+            pltpu.VMEM((128, 2, 4, 768), bf16),
+            pltpu.VMEM((128, 2, 128), bf16),
             dma((10,)),
             dma((2,)),
             dma((2,)),
             dma((2, 3)),
             dma((2, 3, 2)),
+            dma((3,)),
             dma((2,)),
-            dma,
-            dma,
+            dma((2,)),
         ],
         compiler_params=pltpu.CompilerParams(
             collective_id=1, has_side_effects=True, vmem_limit_bytes=60 << 20
@@ -622,11 +637,13 @@
     gathered, normed, token_share = gather_weights(
         w_qkv, w_out.T, norm_gain.reshape(-1, 128), tokens
     )
-    arrived = finish(
+    arrived, ends = finish(
         normed, token_share, q_gain.reshape(1, -1), k_gain.reshape(1, -1),
         grids.T, owners.reshape(1, -1), proj_gain, proj_bias, gathered,
     )
-    return arrived.reshape(-1, 4, SHARE)
+    return jnp.concatenate(
+        [arrived.reshape(-1, 4, 768), ends.reshape(-1, 4, 32)], axis=2
+    )
 
 
 def solution(mesh):

time: 150 us -> 148 us (0.987)
  Pallas kernels: 146 us -> 143 us
    pallas_call x1, Pallas kernels: 87.3 us -> 84.4 us  [finish(): pl.pallas_call(finish_kernel, out_shape=(jax.ShapeDtypeStruct((128, 2, 4,...]
    reshape x1 -> x3, local copies, waits for them, and re-layouts: 4.02 us -> 2.99 us  [the longest x1 2.7 us: body(): arrived.reshape(-1, 4, 768)]
where the time goes in v7:
time: 148 us; the launch traced here: 147 us
  Pallas kernels  143 us (97%)
  local copies, waits for them, and re-layouts  2.99 us (2%)
    pallas_call x1, Pallas kernels, finish(): pl.pallas_call(finish_kernel, out_shape=(jax.ShapeDtypeStruct((128, 2, 4,...  84.4 us
    pallas_call x1, Pallas kernels, gather_weights(): pl.pallas_call(gather_kernel, out_shape=(jax.ShapeDtypeStruct((lax.axis_s...  58.6 us

profile of v7, /device:TPU:1, one launch (start us, length us, event | category | flops | bytes accessed | tf_op | source)
XLA Modules:
  0.0 147.4 jit_solution(17821268260106629975)
XLA Ops:
  0.0 58.6 %gather_weights.1 = (bf16[128,400,128]{2,1,0:T(8,128)(2,1)}, bf16[384,3200]{1,0:T(8,128)(2,1)}, bf16[800,384]{1,0:T(8,128)(2,1)}) custom-call(bf16[25,1536]{1,0:T(8,128)(2,1)} %w_qkv.1, bf16[25,512]{1,0:T(8,128)(2,1)} %bitcast.8, f32[25,128]{1,0:T(8,128)} %bitcast.9, bf16[384,3200]{1,0:T(8,128)(2,1)} %tokens.1), custom_call_target="tpu_custom_call" | custom-call | tf_op jit(solution)/shard_map/gather_weights/pallas_call | solution.py:193
  58.6 84.4 %finish.1 = (bf16[128,2,4,768]{3,2,1,0:T(4,128)(2,1)}, bf16[128,2,128]{2,1,0:T(2,128)(2,1)}) custom-call(bf16[384,3200]{1,0:T(8,128)(2,1)} %get-tuple-element.10.x_hbm, bf16[800,384]{1,0:T(8,128)(2,1)} %get-tuple-element.11.share_hbm, f32[1,512]{1,0:T(1,128)} %bitcast.10, f32[1,512]{1,0:T(1,128)} %bitcast.11, s32[2,3]{1,0:T(2,128)} %bitcast.12, ...), custom_call_target="tpu_custom_call" | custom-call | tf_op jit(solution)/shard_map/finish/pallas_call | solution.py:580
  143.1 0.0 copy-start
  143.1 2.7 %copy.13 = bf16[256,4,768]{0,2,1:T(8,128)(2,1)S(1)} copy(bf16[256,4,768]{2,1,0:T(4,128)(2,1)} %bitcast.7) | data formatting | bytes 3145728 | tf_op jit(solution)/shard_map/reshape | solution.py:645
  145.8 0.0 copy-done
  145.8 0.2 reshape.23
  146.0 0.1 copy.14
  146.1 1.3 pad_maximum_fusion
Async XLA Ops:
  143.1 2.7 %copy-start = (bf16[128,2,128]{2,1,0:T(2,128)(2,1)S(1)}, bf16[128,2,128]{2,1,0:T(2,128)(2,1)}, u32[]{:S(2)}) copy-start(bf16[128,2,128]{2,1,0:T(2,128)(2,1)} %get-tuple-element.14) | copy-start | bytes 196612
